TPU v7x, 32 devices: a whole 2x2x4 slice. The times are simulated.
32 devices in a mesh: ctx: 4 (over z), head: 8 (over y, x, core).
Axes of the slice: x: 2, y: 2, z: 4, core: 2. Of those that a mesh axis runs over, the one named last changes fastest.
Arguments:
- query_rows: bfloat16 [1024, 16384], P('ctx', 'head'), may hold values from -5 to 5
- key_rows: bfloat16 [1024, 1024], P('ctx'), may hold values from -5 to 5
- value_rows: bfloat16 [1024, 1024], P('ctx'), may hold values from -6 to 6
- out_grad: bfloat16 [1024, 16384], P('ctx', 'head'), may hold values from -16 to 16
- span_order: int32 [8], replicated, may hold values from 0 to 7, as said below
Outputs:
- attn_out: bfloat16 [1024, 16384], P('ctx', 'head')
- query_grad: bfloat16 [1024, 16384], P('ctx', 'head')
- key_grad: bfloat16 [1024, 1024], P(('ctx', 'head'))
- value_grad: bfloat16 [1024, 1024], P(('ctx', 'head'))
Inputs may be any that keep to these rules, and one draw needn't show every extreme that they name: `span_order`: each of 0 to 7 appears once, and entries 2d and 2d + 1 add up to 7.
All inputs are finite; a program needn't handle non-finite values.
Results may differ from a plain program's by a relative error of at most 0.025.
Values may be sent and summed in bfloat16 or wider, within the bound.
No kernel may reach another device: no remote copies, remote signals or barrier semaphores. Data moves between devices by JAX's collectives and lax.ppermute only.
A program may use at most 64 MiB of HBM per device.

v0:
```python
import math

import jax
import jax.numpy as jnp
from jax import lax
from jax.sharding import PartitionSpec as P

KV_HEADS = 8
HEAD_DIM = 128
GROUP = 16


def per_device(query_rows, key_rows, value_rows, out_grad, span_order):
    n_ctx = lax.axis_size("ctx")
    n_head = lax.axis_size("head")
    tokens = query_rows.shape[0]
    q_heads = query_rows.shape[1] // HEAD_DIM
    span_len = tokens // 2
    seq_len = tokens * n_ctx
    rows_out = tokens // n_head
    replicas = n_head // KV_HEADS
    score_scale = 1.0 / math.sqrt(HEAD_DIM)
    ctx_index = lax.axis_index("ctx")
    head_index = lax.axis_index("head")
    kv_group = head_index * q_heads // GROUP
    key_own = lax.dynamic_slice_in_dim(key_rows, kv_group * HEAD_DIM, HEAD_DIM, 1)
    value_own = lax.dynamic_slice_in_dim(value_rows, kv_group * HEAD_DIM, HEAD_DIM, 1)
    positions = (
        span_order[:, None] * span_len + jnp.arange(span_len, dtype=jnp.int32)[None, :]
    ).reshape(seq_len)
    query_pos = lax.dynamic_slice_in_dim(positions, ctx_index * tokens, tokens)
    queries = query_rows.reshape(tokens, q_heads, HEAD_DIM)
    grads = out_grad.reshape(tokens, q_heads, HEAD_DIM)
    keys_all, values_all = (
        lax.all_gather(key_own, "ctx", axis=0, tiled=True),
        lax.all_gather(value_own, "ctx", axis=0, tiled=True),
    )
    scores = (
        jnp.einsum("thd,kd->htk", queries, keys_all, preferred_element_type=jnp.float32)
        * score_scale
    )
    visible = positions[None, None, :] <= query_pos[None, :, None]
    scores = jnp.where(visible, scores, -jnp.inf)
    row_top = jnp.max(scores, axis=2, keepdims=True)
    log_total = row_top + jnp.log(jnp.sum(jnp.exp(scores - row_top), axis=2, keepdims=True))
    probs = jnp.exp(scores - log_total)
    probs_low = probs.astype(jnp.bfloat16)
    attended = jnp.einsum(
        "htk,kd->thd", probs_low, values_all, preferred_element_type=jnp.float32
    ).astype(jnp.bfloat16)
    row_dots = jnp.sum(grads.astype(jnp.float32) * attended.astype(jnp.float32), axis=2)
    prob_grad = jnp.einsum("thd,kd->htk", grads, values_all, preferred_element_type=jnp.float32)
    score_grad = (probs * (prob_grad - row_dots.T[:, :, None])).astype(jnp.bfloat16)
    query_grads = (
        jnp.einsum("htk,kd->thd", score_grad, keys_all, preferred_element_type=jnp.float32)
        * score_scale
    ).astype(jnp.bfloat16)
    key_part = (
        jnp.einsum("htk,thd->kd", score_grad, queries, preferred_element_type=jnp.float32)
        * score_scale
    )
    value_part = jnp.einsum("htk,thd->kd", probs_low, grads, preferred_element_type=jnp.float32)
    owned_rows = lax.psum_scatter(
        jnp.concatenate([key_part, value_part], axis=1), "ctx", scatter_dimension=0, tiled=True
    )
    incoming = lax.all_to_all(
        owned_rows.reshape(tokens, 1, 2 * HEAD_DIM), "head", split_axis=0, concat_axis=1, tiled=True
    )
    summed = incoming.reshape(rows_out, KV_HEADS, replicas, 2 * HEAD_DIM).sum(axis=2)
    key_grad = summed[:, :, :HEAD_DIM].reshape(rows_out, KV_HEADS * HEAD_DIM).astype(jnp.bfloat16)
    value_grad = summed[:, :, HEAD_DIM:].reshape(rows_out, KV_HEADS * HEAD_DIM).astype(jnp.bfloat16)
    attn_out = attended.reshape(tokens, q_heads * HEAD_DIM)
    query_grad = query_grads.reshape(tokens, q_heads * HEAD_DIM)
    return (attn_out, query_grad, key_grad, value_grad)


def solution(mesh):
    in_specs = (P("ctx", "head"), P("ctx", None), P("ctx", None), P("ctx", "head"), P())
    out_specs = (
        P("ctx", "head"),
        P("ctx", "head"),
        P(("ctx", "head"), None),
        P(("ctx", "head"), None),
    )
    return jax.shard_map(
        per_device, mesh=mesh, in_specs=in_specs, out_specs=out_specs, check_vma=False
    )
```

profile of v0, /device:TPU:1, one launch (start us, length us, event | category | flops | bytes accessed | tf_op | source)
XLA Modules:
  0.0 145.0 jit_solution(2862973266027188605)
XLA Ops:
  7.2 0.0 copy-start
  7.2 0.0 reduce-scatter.2.cloned.1.call-start
  7.2 1.0 copy-done
  8.2 13.3 %all_gather.7 = bf16[1024,128]{1,0:T(8,128)(2,1)S(1)} all-gather(bf16[256,128]{1,0:T(8,128)(2,1)S(1)} %constant_dynamic-slice_fusion), channel_id=1, replica_groups=mesh['ctx'=4,'head'=8] {'ctx'}, dimensions={0}, use_global_device_ids=true | all-gather | bytes 327680 | tf_op jit(solution)/shard_map/all_gather | solution.py:35
  21.5 0.7 broadcast_multiply_fusion
  22.2 0.1 add_bitcast_fusion
  22.3 0.1 dynamic_slice.10
  22.3 0.2 broadcast_compare_fusion
  22.6 1.5 %copy.81 = bf16[256,2048]{0,1:T(8,128)(2,1)S(1)} copy(bf16[256,2048]{1,0:T(8,128)(2,1)} %param.5) | data formatting | bytes 2097152 | tf_op jit(solution)/shard_map/reshape | solution.py:32
  24.1 0.0 copy-start.1
  24.1 7.2 %fusion.3 = (f32[16,256]{1,0:T(8,128)S(1)}, f32[1024,256,16]{1,0,2:T(8,128)}) fusion(pred[256,1024]{0,1:T(8,128)(4,1)S(1)} %broadcast_compare_fusion, bf16[256,16,128]{0,2,1:T(8,128)(2,1)S(1)} %bitcast.77, bf16[1024,128]{1,0:T(8,128)(2,1)S(1)} %all_gather.7), kind=kOutput, calls=%fused_computation.7 | convolution fusion | flops 1086320640 | bytes 18366464 | tf_op jit(solution)/shard_map/thd,kd->htk/dot_general | solution.py:39
  31.2 9.1 %exponential_reduce_fusion = f32[16,256]{1,0:T(8,128)S(1)} fusion(f32[1024,256,16]{1,0,2:T(8,128)} %get-tuple-element.23, f32[16,256]{1,0:T(8,128)S(1)} %get-tuple-element.22, pred[256,1024]{0,1:T(8,128)(4,1)S(1)} %broadcast_compare_fusion), kind=kLoop, calls=%fused_computation.5 | loop fusion | flops 16773120 | bytes 17072128 | tf_op jit(solution)/shard_map/reduce_sum | solution.py:45
  40.3 0.0 copy-done.1
  40.4 1.3 copy.57
  41.7 0.8 constant_dynamic-slice_fusion.1
  42.5 0.1 copy.80
  42.6 11.2 %all_gather.6 = bf16[1024,128]{0,1:T(8,128)(2,1)S(1)} all-gather(bf16[256,128]{0,1:T(8,128)(2,1)S(1)} %copy.80), channel_id=1, replica_groups=mesh['ctx'=4,'head'=8] {'ctx'}, dimensions={0}, use_global_device_ids=true | all-gather | bytes 327680 | tf_op jit(solution)/shard_map/all_gather | solution.py:36
  53.8 0.0 copy-start.2
  53.8 0.0 slice-start
  53.8 0.0 slice-start.1
  53.8 0.0 slice-start.2
  53.8 8.5 %convolution_bitcast_fusion = f32[1024,128]{0,1:T(8,128)S(1)} fusion(bf16[256,16,128]{0,2,1:T(8,128)(2,1)} %bitcast.81, f32[1024,256,16]{1,0,2:T(8,128)} %get-tuple-element.23, f32[16,256]{1,0:T(8,128)S(1)} %log_add_fusion, pred[256,1024]{0,1:T(8,128)(4,1)S(1)} %broadcast_compare_fusion), kind=kOutput, calls=%fused_computation.11 | convolution fusion | flops 1090519040 | bytes 18628608 | tf_op jit(solution)/shard_map/htk,thd->kd/dot_general | solution.py:62
  62.3 0.0 copy-done.2
  62.3 0.0 slice-start.3
  62.3 10.6 %multiply_reduce_fusion = (f32[256,16]{0,1:T(8,128)S(1)}, bf16[128,16,256]{2,0,1:T(8,128)(2,1)S(1)}) fusion(bf16[256,2048]{0,1:T(8,128)(2,1)S(1)} %copy-done.2, f32[1024,256,16]{1,0,2:T(8,128)} %get-tuple-element.23, f32[16,256]{1,0:T(8,128)S(1)} %log_add_fusion, pred[256,1024]{0,1:T(8,128)(4,1)S(1)} %broadcast_compare_fusion, ...), kind=kOutput, calls=%fused_computation.9 | convolution fusion | flops 1093136384 | bytes 19431424 | tf_op jit(solution)/shard_map/htk,kd->thd/dot_general | solution.py:48
  72.9 0.0 slice-done
  72.9 0.0 slice-done.1
  72.9 0.0 slice-done.2
  72.9 0.0 slice-done.3
  72.9 8.7 %fusion.1 = bf16[16,256,1024]{1,2,0:T(8,128)(2,1)} fusion(f32[1024,256,16]{1,0,2:T(8,128)S(1)} %bitcast.76, bf16[256,16,128]{0,2,1:T(8,128)(2,1)} %bitcast.82, f32[16,256]{1,0:T(8,128)S(1)} %bitcast.85, f32[16,256]{1,0:T(8,128)S(1)} %log_add_fusion, pred[256,1024]{0,1:T(8,128)(4,1)S(1)} %broadcast_compare_fusion, bf16[1024,128]{0,1:T(8,128)(2,1)S(1)} %all_gather.6), kind=kOutput, calls=%fused_computation.2 | convolution fusion | flops 1098907648 | bytes 26771456 | tf_op jit(solution)/shard_map/thd,kd->htk/dot_general | solution.py:52
  81.7 6.2 %fusion.4 = f32[1024,128]{0,1:T(8,128)S(1)} fusion(bf16[16,256,1024]{1,2,0:T(8,128)(2,1)} %fusion.1, bf16[256,16,128]{0,2,1:T(8,128)(2,1)S(1)} %bitcast.78), kind=kOutput, calls=%fused_computation.13 | convolution fusion | flops 1073872896 | bytes 9961472 | tf_op jit(solution)/shard_map/htk,thd->kd/dot_general | solution.py:59
  87.8 1.0 pad_maximum_fusion
  88.9 0.0 reduce-scatter.2.cloned.1.call-update
  88.9 33.2 %reduce-scatter.2.cloned.1.call-done = f32[256,256]{0,1:T(8,128)} async-done(((f32[1024,256]{0,1:T(8,128)}), f32[256,256]{0,1:T(8,128)}) %reduce-scatter.2.cloned.1.call-update) | async-done | bytes 262160 | tf_op jit(solution)/shard_map/reduce_scatter | solution.py:63
  122.1 0.5 broadcast.42
  122.6 1.6 %reduce = f32[256,256]{0,1:T(8,128)S(1)} reduce(f32[256,1,256]{0,2,1:T(8,128)} %bitcast.84, bf16[]{:T(256)} %broadcast.42), dimensions={1}, to_apply=%copy.65.reduce_sub_computation | reduce | bytes 524290 | tf_op jit(solution)/shard_map/reshape | solution.py:67
  124.3 0.1 copy.88
  124.4 0.7 reshape.103
  125.1 4.7 %all-to-all-start = ((bf16[8,2,4096]{2,1,0:T(2,128)(2,1)}), bf16[8,2,4096]{2,1,0:T(2,128)(2,1)S(1)}, u32[]{:S(2)}, u32[]{:S(2)}) async-start(bf16[8,2,4096]{2,1,0:T(2,128)(2,1)} %reshape.103), calls=%async_computation.1 | async-start | bytes 262144 | tf_op jit(solution)/shard_map/all_to_all | solution.py:66
  129.8 4.7 %multiply_convert_fusion = bf16[128,16,256]{2,0,1:T(8,128)(2,1)S(1)} fusion(bf16[16,256,1024]{1,2,0:T(8,128)(2,1)} %fusion.1, bf16[1024,128]{1,0:T(8,128)(2,1)S(1)} %all_gather.7), kind=kOutput, calls=%fused_computation.8 | convolution fusion | flops 1074790400 | bytes 9699328 | tf_op jit(solution)/shard_map/htk,kd->thd/dot_general | solution.py:55
  134.4 1.4 copy.70
  135.9 1.4 copy.69
  137.3 0.0 all-to-all-done
  137.3 0.1 reshape.104
  137.5 0.7 copy_bitcast_fusion
  (5 shorter events, 0.1 us)
Async XLA Ops:
  7.2 1.0 copy-start
  7.2 114.9 %reduce-scatter.2.cloned.1.call-start = ((), (), s32[]{:S(2)}) async-start(), calls=%async_computation.2 | async-start | bytes 1310720 | tf_op jit(solution)/shard_map/reduce_scatter | solution.py:63
  24.1 16.3 %copy-start.1 = (bf16[256,2048]{1,0:T(8,128)(2,1)S(1)}, bf16[256,2048]{1,0:T(8,128)(2,1)}, u32[]{:S(2)}) copy-start(bf16[256,2048]{1,0:T(8,128)(2,1)} %param.8) | copy-start | bytes 3145732
  53.8 8.5 %copy-start.2 = (bf16[256,2048]{0,1:T(8,128)(2,1)S(1)}, bf16[256,2048]{0,1:T(8,128)(2,1)}, u32[]{:S(2)}) copy-start(bf16[256,2048]{0,1:T(8,128)(2,1)} %copy.57) | copy-start | bytes 3145732
  53.8 19.1 %slice-start = ((s8[16777216]{0:T(1024)(128)(4,1)}), s8[4194304]{0:T(1024)(128)(4,1)S(1)}, s32[]{:S(2)}) async-start(s8[16777216]{0:T(1024)(128)(4,1)} %bitcast.75), calls=%async_computation.3 | async-start | bytes 8388608
  53.8 19.1 %slice-start.1 = ((s8[16777216]{0:T(1024)(128)(4,1)}), s8[4194304]{0:T(1024)(128)(4,1)S(1)}, s32[]{:S(2)}) async-start(s8[16777216]{0:T(1024)(128)(4,1)} %bitcast.75), calls=%async_computation.4 | async-start | bytes 8388608
  53.8 19.1 %slice-start.2 = ((s8[16777216]{0:T(1024)(128)(4,1)}), s8[4194304]{0:T(1024)(128)(4,1)S(1)}, s32[]{:S(2)}) async-start(s8[16777216]{0:T(1024)(128)(4,1)} %bitcast.75), calls=%async_computation.5 | async-start | bytes 8388608
  62.3 10.6 %slice-start.3 = ((s8[16777216]{0:T(1024)(128)(4,1)}), s8[4194304]{0:T(1024)(128)(4,1)S(1)}, s32[]{:S(2)}) async-start(s8[16777216]{0:T(1024)(128)(4,1)} %bitcast.75), calls=%async_computation.6 | async-start | bytes 8388608
  125.1 12.2 %all-to-all-start = ((bf16[8,2,4096]{2,1,0:T(2,128)(2,1)}), bf16[8,2,4096]{2,1,0:T(2,128)(2,1)S(1)}, u32[]{:S(2)}, u32[]{:S(2)}) async-start(bf16[8,2,4096]{2,1,0:T(2,128)(2,1)} %reshape.103), calls=%async_computation.1 | async-start | bytes 262144 | tf_op jit(solution)/shard_map/all_to_all | solution.py:66
Sparse Core Ops, SparseCore 0:
  89.0 33.0 reduce-scatter.1
where the time goes:
time: 146 us; the launch traced here: 145 us
  matrix products  45.8 us (31%)
  waiting for transfers between devices  33.2 us (23%)
  blocking collectives  24.5 us (17%)
  between operations  14.2 us (10%)
  other arithmetic  12.7 us (9%)
  local copies, waits for them, and re-layouts  9.78 us (7%)
  starting transfers between devices  4.75 us (3%)
    reduce_scatter x1, waiting for transfers between devices, per_device(): lax.psum_scatter(jnp.concatenate([key_part, value_part], axis=1), 'ctx',...  33.2 us
    all_gather x1, blocking collectives, per_device(): lax.all_gather(key_own, 'ctx', axis=0, tiled=True)  13.3 us
    all_gather x1, blocking collectives, per_device(): lax.all_gather(value_own, 'ctx', axis=0, tiled=True)  11.2 us
    dot_general x1, matrix products, per_device(): jnp.einsum('htk,kd->thd', probs_low, values_all, preferred_element_type=j...  10.6 us
    reduce_sum x1, other arithmetic, per_device(): jnp.sum(jnp.exp(scores - row_top), axis=2, keepdims=True)  9.11 us
    dot_general x1, matrix products, per_device(): jnp.einsum('thd,kd->htk', grads, values_all, preferred_element_type=jnp.f...  8.73 us
    dot_general x1, matrix products, per_device(): jnp.einsum('htk,thd->kd', probs_low, grads, preferred_element_type=jnp.fl...  8.48 us
    dot_general x1, matrix products, per_device(): jnp.einsum('thd,kd->htk', queries, keys_all, preferred_element_type=jnp.f...  7.16 us
  transfers between devices with their start and end apart: 2, of which 1 were waited for; matrix products, arithmetic and copies ran while one was open for 5% of the time, Pallas kernels for 0%

commit v1 on v0

v1 whole, which is shorter than its diff:
```python
import functools
import math

import jax
import jax.numpy as jnp
from jax import lax
from jax.experimental import pallas as pl
from jax.experimental.pallas import tpu as pltpu
from jax.sharding import PartitionSpec as P

KV_HEADS = 8
HEAD_DIM = 128
GROUP = 16
F32 = jnp.float32
BF16 = jnp.bfloat16


def dot_nn(a, b):
    return lax.dot_general(a, b, (((1,), (0,)), ((), ())), preferred_element_type=F32)


def dot_nt(a, b):
    return lax.dot_general(a, b, (((1,), (1,)), ((), ())), preferred_element_type=F32)


def attend_kernel(n_ctx, span, heads, meta, q_ref, g_ref, *rest):
    kv_refs = rest[:n_ctx]
    o_ref, dq_ref, dkv_ref = rest[n_ctx : n_ctx + 3]
    k_s, v_s, kt_s, vt_s, dk_s, dv_s, p_s = rest[n_ctx + 3 :]
    d = HEAD_DIM
    tile = 2 * span
    n_tiles = n_ctx + 1
    scale = 1.0 / math.sqrt(d)
    log2e_scale = scale * math.log2(math.e)
    step = pl.program_id(0)
    ctx = meta[2 * n_ctx]

    @pl.when(step == 0)
    def _():
        for r in range(n_ctx):
            src = lax.rem(ctx + r, n_ctx)
            for half in range(2):
                pos = meta[2 * src + half]
                rows = pl.ds(pl.multiple_of(pos * span, span), span)
                kv = kv_refs[r][half * span : (half + 1) * span, :]
                k_s[rows, :] = kv[:, :d]
                v_s[rows, :] = kv[:, d:]
        for t in range(n_ctx):
            rows = slice(t * tile, (t + 1) * tile)
            kt_s[t] = k_s[rows, :].astype(F32).T.astype(BF16)
            vt_s[t] = v_s[rows, :].astype(F32).T.astype(BF16)
        dk_s[...] = jnp.zeros_like(dk_s)
        dv_s[...] = jnp.zeros_like(dv_s)

    first, second = meta[2 * ctx], meta[2 * ctx + 1]
    hi, lo = jnp.maximum(first, second), jnp.minimum(first, second)
    hi_row = pl.multiple_of(jnp.where(first > second, 0, span), span)
    lo_row = pl.multiple_of(span - hi_row, span)
    hi_tiles = (hi + 2) // 2
    sure_hi = (n_ctx + 2) // 2

    def load(ref, row):
        return jnp.concatenate(
            [ref[pl.ds(row, span), h * d : (h + 1) * d] for h in range(heads)], axis=0
        )

    q = {True: load(q_ref, hi_row), False: load(q_ref, lo_row)}
    g = {True: load(g_ref, hi_row), False: load(g_ref, lo_row)}
    width = heads * span
    kinds, key_tiles, flags = [], [], []
    for t in range(n_tiles):
        if t < sure_hi:
            kinds.append(True)
            key_tiles.append(t)
            flags.append(None)
        elif t == n_tiles - 1:
            kinds.append(False)
            key_tiles.append(t - hi_tiles)
            flags.append(None)
        else:
            is_hi = t < hi_tiles
            kinds.append(None)
            key_tiles.append(jnp.where(is_hi, t, t - hi_tiles))
            flags.append(is_hi)

    def pick(t, pair):
        if kinds[t] is None:
            return jnp.where(flags[t], pair[True], pair[False])
        return pair[kinds[t]]

    def rows_of(t):
        kt = key_tiles[t]
        if isinstance(kt, int):
            return pl.ds(kt * tile, tile)
        return pl.ds(pl.multiple_of(kt * tile, tile), tile)

    row_of = {True: hi_row, False: lo_row}

    def operand(t, ref, pair):
        if kinds[t] is None:
            return load(ref, pl.multiple_of(pick(t, row_of), span))
        return pair[kinds[t]]

    diff = lax.broadcasted_iota(jnp.int32, (tile, width), 0) - lax.rem(
        lax.broadcasted_iota(jnp.int32, (tile, width), 1), span
    )
    qs = [operand(t, q_ref, q) for t in range(n_tiles)]
    gs = [operand(t, g_ref, g) for t in range(n_tiles)]

    tops = {True: None, False: None}

    def fold(acc, t, part, op, neutral):
        for kind in (True, False):
            if kinds[t] is None:
                use = flags[t] if kind else jnp.logical_not(flags[t])
                term = jnp.where(use, part, neutral)
            elif kinds[t] == kind:
                term = part
            else:
                continue
            acc[kind] = term if acc[kind] is None else op(acc[kind], term)

    for t in range(n_tiles):
        s = dot_nt(k_s[rows_of(t), :], qs[t])
        if t >= sure_hi - 1:
            limit = pick(t, {True: hi, False: lo}) * span - key_tiles[t] * tile
            s = jnp.where(diff <= limit, s, -jnp.inf)
        p_s[t] = s
        fold(tops, t, jnp.max(s, axis=0, keepdims=True), jnp.maximum, -jnp.inf)
    sums = {True: None, False: None}
    for t in range(n_tiles):
        p = jnp.exp2((p_s[t] - pick(t, tops)) * log2e_scale)
        p_s[t] = p
        fold(sums, t, jnp.sum(p, axis=0, keepdims=True), jnp.add, 0.0)
    inverse = {kind: 1.0 / sums[kind] for kind in (True, False)}
    outs = {True: None, False: None}
    for t in range(n_tiles):
        p = p_s[t] * pick(t, inverse)
        p_s[t] = p
        p_low = p.astype(BF16)
        fold(outs, t, dot_nn(vt_s[key_tiles[t]], p_low), jnp.add, 0.0)
        dv_s[rows_of(t), :] += dot_nn(p_low, gs[t])
    dots = {}
    for kind in (True, False):
        parts = []
        for h in range(heads):
            cols = slice(h * span, (h + 1) * span)
            o = outs[kind][:, cols].T.astype(BF16)
            o_ref[pl.ds(row_of[kind], span), h * d : (h + 1) * d] = o
            prod = g[kind][cols, :].astype(F32) * o.astype(F32)
            parts.append(jnp.sum(prod.T, axis=0, keepdims=True))
        dots[kind] = jnp.concatenate(parts, axis=1)
    dqs = {True: None, False: None}
    for t in range(n_tiles):
        dp = dot_nt(v_s[rows_of(t), :], gs[t])
        ds = (p_s[t] * (dp - pick(t, dots))).astype(BF16)
        fold(dqs, t, dot_nn(kt_s[key_tiles[t]], ds), jnp.add, 0.0)
        dk_s[rows_of(t), :] += dot_nn(ds, qs[t])
    for kind in (True, False):
        for h in range(heads):
            cols = slice(h * span, (h + 1) * span)
            dq = (dqs[kind][:, cols] * scale).T.astype(BF16)
            dq_ref[pl.ds(row_of[kind], span), h * d : (h + 1) * d] = dq

    @pl.when(step == pl.num_programs(0) - 1)
    def _():
        for i in range(2 * n_ctx):
            rows = pl.ds(pl.multiple_of(meta[i] * span, span), span)
            dkv_ref[i * span : (i + 1) * span, :d] = (dk_s[rows, :] * scale).astype(BF16)
            dkv_ref[i * span : (i + 1) * span, d:] = dv_s[rows, :].astype(BF16)


def attend(meta, q, g, kvs, n_ctx, heads):
    tokens, width = q.shape
    span = tokens // 2
    steps = width // (heads * HEAD_DIM)
    keys = tokens * n_ctx
    d = HEAD_DIM
    col = pl.BlockSpec((tokens, heads * d), lambda i, m: (0, i))
    whole = pl.BlockSpec((tokens, 2 * d), lambda i, m: (0, 0))
    flops = 6 * 2 * (width // d) * tokens // 2 * (n_ctx + 1) * tokens * d
    return pl.pallas_call(
        functools.partial(attend_kernel, n_ctx, span, heads),
        grid_spec=pltpu.PrefetchScalarGridSpec(
            num_scalar_prefetch=1,
            grid=(steps,),
            in_specs=[col, col] + [whole] * n_ctx,
            out_specs=[col, col, pl.BlockSpec((keys, 2 * d), lambda i, m: (0, 0))],
            scratch_shapes=[
                pltpu.VMEM((keys, d), BF16),
                pltpu.VMEM((keys, d), BF16),
                pltpu.VMEM((n_ctx, d, tokens), BF16),
                pltpu.VMEM((n_ctx, d, tokens), BF16),
                pltpu.VMEM((keys, d), F32),
                pltpu.VMEM((keys, d), F32),
                pltpu.VMEM((n_ctx + 1, tokens, heads * span), F32),
            ],
        ),
        out_shape=[
            jax.ShapeDtypeStruct(q.shape, BF16),
            jax.ShapeDtypeStruct(q.shape, BF16),
            jax.ShapeDtypeStruct((keys, 2 * d), BF16),
        ],
        cost_estimate=pl.CostEstimate(
            flops=flops, bytes_accessed=8 * q.size, transcendentals=0
        ),
        name="attend",
    )(meta, q, g, *kvs)


def total_kernel(x_ref, dk_ref, dv_ref):
    n_ctx, groups, replicas = x_ref.shape[:3]
    d = HEAD_DIM
    for k in range(groups):
        acc = None
        for c in range(n_ctx):
            for r in range(replicas):
                part = x_ref[c, k, r].astype(F32)
                acc = part if acc is None else acc + part
        dk_ref[:, k * d : (k + 1) * d] = acc[:, :d].astype(BF16)
        dv_ref[:, k * d : (k + 1) * d] = acc[:, d:].astype(BF16)


def total(x, rows_out):
    shape = jax.ShapeDtypeStruct((rows_out, KV_HEADS * HEAD_DIM), BF16)
    return pl.pallas_call(total_kernel, out_shape=[shape, shape], name="total")(x)


def per_device(query_rows, key_rows, value_rows, out_grad, span_order):
    n_ctx = lax.axis_size("ctx")
    n_head = lax.axis_size("head")
    tokens = query_rows.shape[0]
    q_heads = query_rows.shape[1] // HEAD_DIM
    rows_out = tokens // n_head
    replicas = n_head // KV_HEADS
    ctx_index = lax.axis_index("ctx")
    head_index = lax.axis_index("head")
    kv_group = head_index * q_heads // GROUP
    own = jnp.concatenate(
        [
            lax.dynamic_slice_in_dim(a, kv_group * HEAD_DIM, HEAD_DIM, 1)
            for a in (key_rows, value_rows)
        ],
        axis=1,
    )
    kvs = [own]
    for r in range(1, n_ctx):
        kvs.append(lax.ppermute(own, "ctx", [((i + r) % n_ctx, i) for i in range(n_ctx)]))
    meta = jnp.concatenate([span_order, ctx_index[None].astype(jnp.int32)])
    heads = math.gcd(q_heads, HEADS)
    attn_out, query_grad, partial = attend(meta, query_rows, out_grad, kvs, n_ctx, heads)
    parts = lax.all_to_all(
        partial.reshape(n_ctx * n_head, rows_out, 2 * HEAD_DIM),
        ("ctx", "head"),
        split_axis=0,
        concat_axis=0,
    )
    parts = parts.reshape(n_ctx, KV_HEADS, replicas, rows_out, 2 * HEAD_DIM)
    key_grad, value_grad = total(parts, rows_out)
    return (attn_out, query_grad, key_grad, value_grad)


HEADS = 4


def solution(mesh):
    in_specs = (P("ctx", "head"), P("ctx", None), P("ctx", None), P("ctx", "head"), P())
    out_specs = (
        P("ctx", "head"),
        P("ctx", "head"),
        P(("ctx", "head"), None),
        P(("ctx", "head"), None),
    )
    return jax.shard_map(
        per_device, mesh=mesh, in_specs=in_specs, out_specs=out_specs, check_vma=False
    )
```

time: 146 us -> 57.9 us (0.40)
  matrix products: 45.8 us -> 0 us
  waiting for transfers between devices: 33.2 us -> 6.98 us
  Pallas kernels: 0 us -> 18 us
  between operations: 14.2 us -> 0.69 us
  other arithmetic: 12.7 us -> 0.6 us
  local copies, waits for them, and re-layouts: 9.78 us -> 2.84 us
  blocking collectives: 24.5 us -> 22.3 us
    dot_general x6 -> x0, matrix products: 45.8 us -> none  [the longest x1 10.6 us: per_device(): jnp.einsum('htk,kd->thd', probs_low, values_all, preferred_element_type=j...]
    reduce_scatter x1 -> x0, waiting for transfers between devices: 33.2 us -> none  [per_device(): lax.psum_scatter(jnp.concatenate([key_part, value_part], axis=1), 'ctx',...]
    all_gather x2 -> x0, blocking collectives: 24.5 us -> none  [the longest x1 13.3 us: per_device(): lax.all_gather(key_own, 'ctx', axis=0, tiled=True)]
    all_to_all x0 -> x1, blocking collectives: none -> 22.3 us  [per_device(): lax.all_to_all(partial.reshape(n_ctx * n_head, rows_out, 2 * HEAD_DIM), (...]
    pallas_call x0 -> x2, Pallas kernels: none -> 18 us  [the longest x1 16.2 us: attend(): pl.pallas_call(functools.partial(attend_kernel, n_ctx, span, heads), grid...]
    reduce_sum x1 -> x0, other arithmetic: 9.11 us -> none  [per_device(): jnp.sum(jnp.exp(scores - row_top), axis=2, keepdims=True)]
    ppermute x0 -> x3, waiting for transfers between devices: none -> 6.98 us  [per_device(): lax.ppermute(own, 'ctx', [((i + r) % n_ctx, i) for i in range(n_ctx)])]
    ppermute x0 -> x3, starting transfers between devices: none -> 5.54 us  [per_device(): lax.ppermute(own, 'ctx', [((i + r) % n_ctx, i) for i in range(n_ctx)])]
  transfers between devices with their start and end apart: 2 -> 3, of which waited for: 1 -> 2; matrix products, arithmetic and copies ran while one was open for 5% -> 1% of each run, Pallas kernels for 0% -> 0%
where the time goes in v1:
time: 57.9 us; the launch traced here: 56.9 us
  blocking collectives  22.3 us (39%)
  Pallas kernels  18 us (31%)
  waiting for transfers between devices  6.98 us (12%)
  starting transfers between devices  5.54 us (10%)
  local copies, waits for them, and re-layouts  2.84 us (5%)
  between operations  0.69 us (1%)
  other arithmetic  0.6 us (1%)
    all_to_all x1, blocking collectives, per_device(): lax.all_to_all(partial.reshape(n_ctx * n_head, rows_out, 2 * HEAD_DIM), (...  22.3 us
    pallas_call x1, Pallas kernels, attend(): pl.pallas_call(functools.partial(attend_kernel, n_ctx, span, heads), grid...  16.2 us
    ppermute x3, waiting for transfers between devices, per_device(): lax.ppermute(own, 'ctx', [((i + r) % n_ctx, i) for i in range(n_ctx)])  6.98 us
    ppermute x3, starting transfers between devices, per_device(): lax.ppermute(own, 'ctx', [((i + r) % n_ctx, i) for i in range(n_ctx)])  5.54 us
    unnamed x10, local copies, waits for them, and re-layouts  1.95 us
    pallas_call x1, Pallas kernels, total(): pl.pallas_call(total_kernel, out_shape=[shape, shape], name='total')(x)  1.76 us
  transfers between devices with their start and end apart: 3, of which 2 were waited for; matrix products, arithmetic and copies ran while one was open for 1% of the time, Pallas kernels for 0%

profile of v1, /device:TPU:1, one launch (start us, length us, event | category | flops | bytes accessed | tf_op | source)
XLA Modules:
  0.0 56.9 jit_solution(1484138816110091229)
XLA Ops:
  0.7 0.9 %constant_dynamic-slice_fusion = (bf16[256,128]{1,0:T(8,128)(2,1)S(1)}, bf16[256,128]{1,0:T(8,128)(2,1)S(1)}) fusion(bf16[256,1024]{1,0:T(8,128)(2,1)} %param.7, s32[]{:T(128)S(6)} %select_n.10, bf16[256,1024]{1,0:T(8,128)(2,1)} %param.6), kind=kLoop, calls=%fused_computation.2 | loop fusion | bytes 262148 | tf_op jit(solution)/shard_map/dynamic_slice | solution.py:241
  1.6 0.0 copy-start
  1.6 2.2 %collective-permute-start.2 = (bf16[256,256]{1,0:T(8,128)(2,1)S(1)}, bf16[256,256]{1,0:T(8,128)(2,1)S(1)}, u32[]{:S(2)}, u32[]{:S(2)}) collective-permute-start(bf16[256,256]{1,0:T(8,128)(2,1)S(1)} %pad_maximum_fusion.rest_0_), channel_id=1, source_target_pairs={{24,0},{0,8},{8,16},{16,24},{25,1},{1,9},{9,17},{17,25},{26,2},{2,... | collective-permute-start | bytes 393224 | tf_op jit(solution)/shard_map/ppermute | solution.py:248
  3.7 2.3 %collective-permute-start.1 = (bf16[256,256]{1,0:T(8,128)(2,1)S(1)}, bf16[256,256]{1,0:T(8,128)(2,1)S(1)}, u32[]{:S(2)}, u32[]{:S(2)}) collective-permute-start(bf16[256,256]{1,0:T(8,128)(2,1)S(1)} %pad_maximum_fusion.rest_0_), channel_id=1, source_target_pairs={{16,0},{24,8},{0,16},{8,24},{17,1},{25,9},{1,17},{9,25},{18,2},{26... | collective-permute-start | bytes 393224 | tf_op jit(solution)/shard_map/ppermute | solution.py:248
  6.1 1.1 %collective-permute-start = (bf16[256,256]{1,0:T(8,128)(2,1)S(1)}, bf16[256,256]{1,0:T(8,128)(2,1)S(1)}, u32[]{:S(2)}, u32[]{:S(2)}) collective-permute-start(bf16[256,256]{1,0:T(8,128)(2,1)S(1)} %pad_maximum_fusion.rest_0_), channel_id=1, source_target_pairs={{8,0},{16,8},{24,16},{0,24},{9,1},{17,9},{25,17},{1,25},{10,2},{18... | collective-permute-start | bytes 393224 | tf_op jit(solution)/shard_map/ppermute | solution.py:248
  7.1 0.0 copy-start.4
  7.1 0.7 %copy-done.4 = s32[8]{0:T(128)S(1)} copy-done((s32[8]{0:T(128)S(1)}, s32[8]{0:T(128)}, u32[]{:S(2)}) %copy-start.4) | copy-done | bytes 56
  7.8 0.6 %pad_add_fusion.meta = s32[9]{0:T(128)} fusion(s32[1]{0:T(128)} %bitcast, s32[8]{0:T(128)S(1)} %copy-done.4), kind=kLoop, calls=%fused_computation.1 | loop fusion | flops 9 | bytes 72 | tf_op jit(solution)/shard_map/concatenate | solution.py:249
  8.4 0.6 %collective-permute-done.2.rest_3_ = bf16[256,256]{1,0:T(8,128)(2,1)S(1)} collective-permute-done((bf16[256,256]{1,0:T(8,128)(2,1)S(1)}, bf16[256,256]{1,0:T(8,128)(2,1)S(1)}, u32[]{:S(2)}, u32[]{:S(2)}) %collective-permute-start.2) | collective-permute-done | bytes 131104 | tf_op jit(solution)/shard_map/ppermute | solution.py:248
  9.0 0.0 copy-start.1
  9.0 6.4 %collective-permute-done.1.rest_2_ = bf16[256,256]{1,0:T(8,128)(2,1)S(1)} collective-permute-done((bf16[256,256]{1,0:T(8,128)(2,1)S(1)}, bf16[256,256]{1,0:T(8,128)(2,1)S(1)}, u32[]{:S(2)}, u32[]{:S(2)}) %collective-permute-start.1) | collective-permute-done | bytes 131104 | tf_op jit(solution)/shard_map/ppermute | solution.py:248
  15.3 0.0 copy-start.2
  15.3 0.0 collective-permute-done.rest_1_
  15.4 0.0 copy-done
  15.4 0.0 copy-done.1
  15.4 0.6 %copy-done.2 = bf16[256,256]{1,0:T(8,128)(2,1)} copy-done((bf16[256,256]{1,0:T(8,128)(2,1)}, bf16[256,256]{1,0:T(8,128)(2,1)S(1)}, u32[]{:S(2)}) %copy-start.2) | copy-done | bytes 131096
  16.0 0.0 copy-start.3
  16.0 0.6 %copy-done.3 = bf16[256,256]{1,0:T(8,128)(2,1)} copy-done((bf16[256,256]{1,0:T(8,128)(2,1)}, bf16[256,256]{1,0:T(8,128)(2,1)S(1)}, u32[]{:S(2)}) %copy-start.3) | copy-done | bytes 131096
  16.7 16.2 %attend.1 = (bf16[256,2048]{1,0:T(8,128)(2,1)}, bf16[256,2048]{1,0:T(8,128)(2,1)}, bf16[1024,256]{1,0:T(8,128)(2,1)}) custom-call(s32[9]{0:T(128)} %pad_add_fusion.meta, bf16[256,2048]{1,0:T(8,128)(2,1)} %q_ref.1, bf16[256,2048]{1,0:T(8,128)(2,1)} %g_ref.1, bf16[256,256]{1,0:T(8,128)(2,1)} %copy-done, bf16[256,256]{1,0:T(8,128)(2,1)} %copy-done.3, ...), custom_call_target="tpu_custom_call" | custom-call | flops 4026531840 | bytes 4194304 | tf_op jit(solution)/shard_map/attend/pallas_call | solution.py:182
  32.9 22.3 %all_to_all.5 = bf16[32,32,256]{2,1,0:T(8,128)(2,1)} all-to-all(bf16[32,32,256]{2,1,0:T(8,128)(2,1)} %bitcast.4), channel_id=1, replica_groups=mesh['ctx'=4,'head'=8] {'ctx','head'}, dimensions={0} | all-to-all | bytes 1048576 | tf_op jit(solution)/shard_map/all_to_all | solution.py:252
  55.2 1.8 %total.1 = (bf16[32,1024]{1,0:T(8,128)(2,1)}, bf16[32,1024]{1,0:T(8,128)(2,1)}) custom-call(bf16[4,8,1,32,256]{4,3,2,1,0:T(8,128)(2,1)} %bitcast.3), custom_call_target="tpu_custom_call" | custom-call | tf_op jit(solution)/shard_map/total/pallas_call | solution.py:226
  (1 shorter events, 0.0 us)
Async XLA Ops:
  1.6 13.8 %copy-start = (bf16[256,256]{1,0:T(8,128)(2,1)}, bf16[256,256]{1,0:T(8,128)(2,1)S(1)}, u32[]{:S(2)}) copy-start(bf16[256,256]{1,0:T(8,128)(2,1)S(1)} %pad_maximum_fusion.rest_0_) | copy-start | bytes 393220
  1.6 7.4 %collective-permute-start.2 = (bf16[256,256]{1,0:T(8,128)(2,1)S(1)}, bf16[256,256]{1,0:T(8,128)(2,1)S(1)}, u32[]{:S(2)}, u32[]{:S(2)}) collective-permute-start(bf16[256,256]{1,0:T(8,128)(2,1)S(1)} %pad_maximum_fusion.rest_0_), channel_id=1, source_target_pairs={{24,0},{0,8},{8,16},{16,24},{25,1},{1,9},{9,17},{17,25},{26,2},{2,... | collective-permute-start | bytes 393224 | tf_op jit(solution)/shard_map/ppermute | solution.py:248
  3.7 11.6 %collective-permute-start.1 = (bf16[256,256]{1,0:T(8,128)(2,1)S(1)}, bf16[256,256]{1,0:T(8,128)(2,1)S(1)}, u32[]{:S(2)}, u32[]{:S(2)}) collective-permute-start(bf16[256,256]{1,0:T(8,128)(2,1)S(1)} %pad_maximum_fusion.rest_0_), channel_id=1, source_target_pairs={{16,0},{24,8},{0,16},{8,24},{17,1},{25,9},{1,17},{9,25},{18,2},{26... | collective-permute-start | bytes 393224 | tf_op jit(solution)/shard_map/ppermute | solution.py:248
  6.1 9.3 %collective-permute-start = (bf16[256,256]{1,0:T(8,128)(2,1)S(1)}, bf16[256,256]{1,0:T(8,128)(2,1)S(1)}, u32[]{:S(2)}, u32[]{:S(2)}) collective-permute-start(bf16[256,256]{1,0:T(8,128)(2,1)S(1)} %pad_maximum_fusion.rest_0_), channel_id=1, source_target_pairs={{8,0},{16,8},{24,16},{0,24},{9,1},{17,9},{25,17},{1,25},{10,2},{18... | collective-permute-start | bytes 393224 | tf_op jit(solution)/shard_map/ppermute | solution.py:248
  7.1 0.7 %copy-start.4 = (s32[8]{0:T(128)S(1)}, s32[8]{0:T(128)}, u32[]{:S(2)}) copy-start(s32[8]{0:T(128)} %param.9) | copy-start | bytes 100
  9.0 6.4 %copy-start.1 = (bf16[256,256]{1,0:T(8,128)(2,1)}, bf16[256,256]{1,0:T(8,128)(2,1)S(1)}, u32[]{:S(2)}) copy-start(bf16[256,256]{1,0:T(8,128)(2,1)S(1)} %collective-permute-done.2.rest_3_) | copy-start | bytes 393220
  15.3 0.7 %copy-start.2 = (bf16[256,256]{1,0:T(8,128)(2,1)}, bf16[256,256]{1,0:T(8,128)(2,1)S(1)}, u32[]{:S(2)}) copy-start(bf16[256,256]{1,0:T(8,128)(2,1)S(1)} %collective-permute-done.1.rest_2_) | copy-start | bytes 393220
  16.0 0.6 %copy-start.3 = (bf16[256,256]{1,0:T(8,128)(2,1)}, bf16[256,256]{1,0:T(8,128)(2,1)S(1)}, u32[]{:S(2)}) copy-start(bf16[256,256]{1,0:T(8,128)(2,1)S(1)} %collective-permute-done.rest_1_) | copy-start | bytes 393220

commit v2 on v0

v2 whole, which is shorter than its diff:
```python
import functools
import math

import jax
import jax.numpy as jnp
from jax import lax
from jax.experimental import pallas as pl
from jax.experimental.pallas import tpu as pltpu
from jax.sharding import PartitionSpec as P


KV_HEADS = 8
HEAD_DIM = 128
GROUP = 16
HEADS = 8
VMEM_BYTES = 24 << 20
COVER = 20_000_000_000
F32 = jnp.float32
BF16 = jnp.bfloat16
SCALE = 1.0 / math.sqrt(HEAD_DIM)
EXP_SCALE = SCALE * math.log2(math.e)


def dot_nn(a, b):
    return lax.dot_general(a, b, (((1,), (0,)), ((), ())), preferred_element_type=F32)


def dot_nt(a, b):
    return lax.dot_general(a, b, (((1,), (1,)), ((), ())), preferred_element_type=F32)


def partner(ctx, r, n_ctx):
    return ctx ^ r if n_ctx & (n_ctx - 1) == 0 else (ctx + r) % n_ctx


class Plan:
    def __init__(self, n_ctx, span, meta):
        self.n_ctx, self.span, self.meta = n_ctx, span, meta
        self.tile = 2 * span
        self.slots = n_ctx + 1
        self.ctx = lax.axis_index("ctx")
        first, second = meta[2 * self.ctx], meta[2 * self.ctx + 1]
        self.hi, self.lo = jnp.maximum(first, second), jnp.minimum(first, second)
        hi_row = pl.multiple_of(jnp.where(first > second, 0, span), span)
        self.row = {True: hi_row, False: pl.multiple_of(span - hi_row, span)}
        self.hi_tiles = (self.hi + 2) // 2
        self.sure_hi = (n_ctx + 2) // 2

    def kind(self, t):
        if t < self.sure_hi:
            return True
        return False if t == self.slots - 1 else None

    def is_hi(self, t):
        return t < self.hi_tiles

    def key_tile(self, t):
        kind = self.kind(t)
        if kind:
            return t
        if kind is None:
            return jnp.where(self.is_hi(t), t, t - self.hi_tiles)
        return t - self.hi_tiles

    def keys(self, t):
        return pl.ds(pl.multiple_of(self.key_tile(t) * self.tile, self.tile), self.tile)

    def pick(self, t, pair):
        kind = self.kind(t)
        if kind is None:
            return jnp.where(self.is_hi(t), pair[True], pair[False])
        return pair[kind]

    def fold(self, acc, t, part, op, neutral):
        for kind in (True, False):
            if self.kind(t) is None:
                use = self.is_hi(t) if kind else jnp.logical_not(self.is_hi(t))
                term = jnp.where(use, part, neutral)
            elif self.kind(t) == kind:
                term = part
            else:
                continue
            acc[kind] = term if acc[kind] is None else op(acc[kind], term)

    def sort(self, shards, out):
        for r, shard in enumerate(shards):
            src = partner(self.ctx, r, self.n_ctx)
            for half in range(2):
                pos = self.meta[2 * src + half]
                rows = pl.ds(pl.multiple_of(pos * self.span, self.span), self.span)
                out[rows, :] = shard[half * self.span : (half + 1) * self.span, :]

    def unsort(self, total, outs):
        for r, out in enumerate(outs):
            dest = partner(self.ctx, r, self.n_ctx)
            for half in range(2):
                pos = self.meta[2 * dest + half]
                rows = pl.ds(pl.multiple_of(pos * self.span, self.span), self.span)
                out[half * self.span : (half + 1) * self.span, :] = total(rows)

    def queries(self, ref, row, cols):
        return jnp.concatenate(
            [
                ref[pl.ds(row, self.span), c : c + HEAD_DIM]
                for c in range(cols.start, cols.stop, HEAD_DIM)
            ],
            axis=0,
        )

    def slot_queries(self, ref, cols):
        pair = {k: self.queries(ref, self.row[k], cols) for k in (True, False)}
        out = []
        for t in range(self.slots):
            if self.kind(t) is None:
                row = pl.multiple_of(self.pick(t, self.row), self.span)
                out.append(self.queries(ref, row, cols))
            else:
                out.append(pair[self.kind(t)])
        return pair, out


def groups(width, heads):
    step = heads * HEAD_DIM
    return [slice(c, c + step) for c in range(0, width, step)]


def own_kernel(kv_ref, k_ref, v_ref):
    tokens = k_ref.shape[0]
    k_ref[...] = kv_ref[:tokens, :]
    v_ref[...] = kv_ref[tokens:, :]


def split_own(own):
    vmem = pl.BlockSpec(memory_space=pltpu.VMEM)
    shape = jax.ShapeDtypeStruct((own.shape[0] // 2, own.shape[1]), BF16)
    return pl.pallas_call(
        own_kernel,
        in_specs=[vmem],
        out_specs=[vmem, vmem],
        out_shape=[shape, shape],
        cost_estimate=pl.CostEstimate(flops=COVER, bytes_accessed=0, transcendentals=0),
        compiler_params=pltpu.CompilerParams(vmem_limit_bytes=VMEM_BYTES),
        name="own",
    )(own)


def forward_kernel(n_ctx, span, heads, meta, q_ref, g_ref, *rest):
    shards = rest[:n_ctx]
    p_ref, inv_ref, gs_ref, k_ref = rest[n_ctx : n_ctx + 4]
    dv_refs = rest[n_ctx + 4 : 2 * n_ctx + 4]
    s_ref, acc_ref = rest[2 * n_ctx + 4 :]
    plan = Plan(n_ctx, span, meta)
    d = HEAD_DIM
    plan.sort(shards, k_ref)
    acc_ref[...] = jnp.zeros_like(acc_ref)
    width = heads * span
    diff = lax.broadcasted_iota(jnp.int32, (plan.tile, width), 0) - lax.rem(
        lax.broadcasted_iota(jnp.int32, (plan.tile, width), 1), span
    )
    for cols in groups(q_ref.shape[1], heads):
        _, qs = plan.slot_queries(q_ref, cols)
        tops = {True: None, False: None}
        for t in range(plan.slots):
            s = dot_nt(k_ref[plan.keys(t), :], qs[t])
            if t >= plan.sure_hi - 1:
                position = plan.pick(t, {True: plan.hi, False: plan.lo})
                limit = position * span - plan.key_tile(t) * plan.tile
                s = jnp.where(diff <= limit, s, -jnp.inf)
            s_ref[t, :, cols] = s
            plan.fold(tops, t, jnp.max(s, axis=0, keepdims=True), jnp.maximum, -jnp.inf)
        sums = {True: None, False: None}
        for t in range(plan.slots):
            p = jnp.exp2((s_ref[t, :, cols] - plan.pick(t, tops)) * EXP_SCALE)
            p_ref[t, :, cols] = p.astype(BF16)
            plan.fold(sums, t, jnp.sum(p, axis=0, keepdims=True), jnp.add, 0.0)
        for kind, r in ((True, 0), (False, 1)):
            inverse = 1.0 / sums[kind]
            inv_ref[r : r + 1, cols] = inverse
            for h in range(heads):
                here = slice(cols.start + h * d, cols.start + (h + 1) * d)
                row = inverse[:, h * span : (h + 1) * span]
                column = jnp.broadcast_to(row, (span, span)).T
                g = g_ref[pl.ds(plan.row[kind], span), here].astype(F32)
                gs_ref[pl.ds(plan.row[kind], span), here] = (g * column).astype(BF16)
        _, gs = plan.slot_queries(gs_ref, cols)
        for t in range(plan.slots):
            acc_ref[plan.keys(t), :] += dot_nn(p_ref[t, :, cols], gs[t])
    plan.unsort(lambda rows: acc_ref[rows, :].astype(BF16), dv_refs)


def backward_kernel(n_ctx, span, heads, meta, p_ref, inv_ref, gs_ref, q_ref, *rest):
    shards = rest[:n_ctx]
    o_ref, ds_ref = rest[n_ctx : n_ctx + 2]
    dk_refs = rest[n_ctx + 2 : 2 * n_ctx + 2]
    v_ref, vt_ref, acc_ref = rest[2 * n_ctx + 2 :]
    plan = Plan(n_ctx, span, meta)
    d = HEAD_DIM
    plan.sort(shards, v_ref)
    for t in range(n_ctx):
        vt_ref[t] = v_ref[t * plan.tile : (t + 1) * plan.tile, :].astype(F32).T.astype(BF16)
    acc_ref[...] = jnp.zeros_like(acc_ref)
    for cols in groups(q_ref.shape[1], heads):
        _, qs = plan.slot_queries(q_ref, cols)
        _, gs = plan.slot_queries(gs_ref, cols)
        outs = {True: None, False: None}
        for t in range(plan.slots):
            part = dot_nn(vt_ref[plan.key_tile(t)], p_ref[t, :, cols])
            plan.fold(outs, t, part, jnp.add, 0.0)
        dots = {}
        for kind, r in ((True, 0), (False, 1)):
            out = outs[kind] * inv_ref[r : r + 1, cols]
            parts = []
            for h in range(heads):
                here = slice(cols.start + h * d, cols.start + (h + 1) * d)
                o = out[:, h * span : (h + 1) * span].T.astype(BF16)
                o_ref[pl.ds(plan.row[kind], span), here] = o
                g = gs_ref[pl.ds(plan.row[kind], span), here].astype(F32)
                parts.append(jnp.sum((g * o.astype(F32)).T, axis=0, keepdims=True))
            dots[kind] = jnp.concatenate(parts, axis=1)
        for t in range(plan.slots):
            dp = dot_nt(v_ref[plan.keys(t), :], gs[t])
            ds = (p_ref[t, :, cols].astype(F32) * (dp - plan.pick(t, dots))).astype(BF16)
            ds_ref[t, :, cols] = ds
            acc_ref[plan.keys(t), :] += dot_nn(ds, qs[t])
    plan.unsort(lambda rows: (acc_ref[rows, :] * SCALE).astype(BF16), dk_refs)


def query_kernel(n_ctx, span, heads, meta, ds_ref, k_ref, dq_ref, kt_ref):
    plan = Plan(n_ctx, span, meta)
    d = HEAD_DIM
    for t in range(n_ctx):
        kt_ref[t] = k_ref[t * plan.tile : (t + 1) * plan.tile, :].astype(F32).T.astype(BF16)
    for cols in groups(dq_ref.shape[1], heads):
        dqs = {True: None, False: None}
        for t in range(plan.slots):
            part = dot_nn(kt_ref[plan.key_tile(t)], ds_ref[t, :, cols])
            plan.fold(dqs, t, part, jnp.add, 0.0)
        for kind in (True, False):
            for h in range(heads):
                here = slice(cols.start + h * d, cols.start + (h + 1) * d)
                dq = (dqs[kind][:, h * span : (h + 1) * span] * SCALE).T.astype(BF16)
                dq_ref[pl.ds(plan.row[kind], span), here] = dq


def call(body, out_shape, scratch, flops):
    vmem = pl.BlockSpec(memory_space=pltpu.VMEM)

    def run(meta, *args):
        return pl.pallas_call(
            body,
            in_specs=[pl.BlockSpec(memory_space=pltpu.SMEM)] + [vmem] * len(args),
            out_specs=[vmem] * len(out_shape),
            out_shape=out_shape,
            scratch_shapes=scratch,
            cost_estimate=pl.CostEstimate(
                flops=flops, bytes_accessed=flops // 512, transcendentals=0
            ),
            compiler_params=pltpu.CompilerParams(vmem_limit_bytes=VMEM_BYTES),
        )(meta, *args)

    return run


def per_device(query_rows, key_rows, value_rows, out_grad, span_order):
    n_ctx = lax.axis_size("ctx")
    n_head = lax.axis_size("head")
    tokens, width = query_rows.shape
    span = tokens // 2
    keys = tokens * n_ctx
    d = HEAD_DIM
    q_heads = width // d
    rows_out = tokens // n_head
    replicas = n_head // KV_HEADS
    heads = math.gcd(q_heads, HEADS)

    def shift(a, r, back=False):
        pairs = [(partner(i, r, n_ctx), i) for i in range(n_ctx)]
        return lax.ppermute(a, "ctx", [p[::-1] for p in pairs] if back else pairs)

    def shape(dims, dtype=BF16):
        return jax.ShapeDtypeStruct(dims, dtype)

    others = range(1, n_ctx)
    kv_group = lax.axis_index("head") * q_heads // GROUP
    own = lax.optimization_barrier(
        jnp.concatenate(
            [lax.dynamic_slice_in_dim(a, kv_group * d, d, 1) for a in (key_rows, value_rows)]
        )
    )
    key_own, value_own = split_own(own)

    def gather(own, name):
        if n_ctx != 4 or name == "value":
            return [own] + [shift(own, r) for r in others]
        near, far = shift(own, 1), shift(own, 2)
        across = lax.ppermute(far, "ctx", [(i ^ 1, i) for i in range(n_ctx)])
        return [own, near, far, across]

    key_shards, value_shards = gather(key_own, "key"), gather(value_own, "value")
    slots = (n_ctx + 1, tokens, q_heads * span)
    rows, pair, shard = shape((tokens, width)), shape((2, q_heads * span), F32), shape((tokens, d))
    work = 2 * slots[0] * slots[1] * slots[2] * d
    bind = lambda f: functools.partial(f, n_ctx, span, heads)
    p, inverse, grads, key_sorted, *value_parts = call(
        bind(forward_kernel),
        [shape(slots), pair, rows, shape((keys, d))] + [shard] * n_ctx,
        [pltpu.VMEM(slots, F32), pltpu.VMEM((keys, d), F32)], 2 * work,
    )(span_order, query_rows, out_grad, *key_shards)
    attn_out, score_grads, *key_parts = call(
        bind(backward_kernel), [rows, shape(slots)] + [shard] * n_ctx,
        [
            pltpu.VMEM((keys, d), BF16),
            pltpu.VMEM((n_ctx, d, tokens), BF16),
            pltpu.VMEM((keys, d), F32),
        ], 3 * work,
    )(span_order, p, inverse, grads, query_rows, *value_shards)
    (query_grad,) = call(
        bind(query_kernel), [rows],
        [pltpu.VMEM((n_ctx, d, tokens), BF16)], work,
    )(span_order, score_grads, key_sorted)

    def scatter(parts, name):
        if n_ctx == 4 and name == "value_grad":
            given = jnp.concatenate([parts[1], parts[3]])
            taken = shift(given, 1).astype(F32)
            far = (parts[2].astype(F32) + taken[tokens:]).astype(BF16)
            far = shift(far, 2).astype(F32)
            return (parts[0].astype(F32) + taken[:tokens] + far).astype(BF16)
        total = parts[0].astype(F32)
        for r in others:
            total += shift(parts[r], r, True).astype(F32)
        return total.astype(BF16)

    value_sum, key_sum = scatter(value_parts, "value_grad"), scatter(key_parts, "key_grad")
    owned = jnp.concatenate([key_sum, value_sum], axis=1)
    parts = lax.all_to_all(
        owned.reshape(n_head, rows_out, 2 * d), "head", split_axis=0, concat_axis=0
    )
    key_grad, value_grad = total(parts.reshape(KV_HEADS, replicas, rows_out, 2 * d), rows_out)
    return (attn_out, query_grad, key_grad, value_grad)


def total_kernel(x_ref, dk_ref, dv_ref):
    d = HEAD_DIM
    for k in range(x_ref.shape[0]):
        acc = x_ref[k, 0].astype(F32)
        for r in range(1, x_ref.shape[1]):
            acc += x_ref[k, r].astype(F32)
        dk_ref[:, k * d : (k + 1) * d] = acc[:, :d].astype(BF16)
        dv_ref[:, k * d : (k + 1) * d] = acc[:, d:].astype(BF16)


def total(x, rows_out):
    shape = jax.ShapeDtypeStruct((rows_out, KV_HEADS * HEAD_DIM), BF16)
    return pl.pallas_call(
        total_kernel,
        out_shape=[shape, shape],
        compiler_params=pltpu.CompilerParams(vmem_limit_bytes=VMEM_BYTES),
        name="total",
    )(x)


def solution(mesh):
    in_specs = (P("ctx", "head"), P("ctx", None), P("ctx", None), P("ctx", "head"), P())
    out_specs = (
        P("ctx", "head"),
        P("ctx", "head"),
        P(("ctx", "head"), None),
        P(("ctx", "head"), None),
    )

    return jax.shard_map(
        per_device, mesh=mesh, in_specs=in_specs, out_specs=out_specs, check_vma=False
    )
```

time: 146 us -> 53.5 us (0.37)
  matrix products: 45.8 us -> 0 us
  waiting for transfers between devices: 33.2 us -> 7.55 us
  blocking collectives: 24.5 us -> 0 us
  starting transfers between devices: 4.75 us -> 21.8 us
  Pallas kernels: 0 us -> 16.2 us
  between operations: 14.2 us -> 0.76 us
  other arithmetic: 12.7 us -> 0.82 us
  local copies, waits for them, and re-layouts: 9.78 us -> 5.72 us
    dot_general x6 -> x0, matrix products: 45.8 us -> none  [the longest x1 10.6 us: per_device(): jnp.einsum('htk,kd->thd', probs_low, values_all, preferred_element_type=j...]
    reduce_scatter x1 -> x0, waiting for transfers between devices: 33.2 us -> none  [per_device(): lax.psum_scatter(jnp.concatenate([key_part, value_part], axis=1), 'ctx',...]
    all_gather x2 -> x0, blocking collectives: 24.5 us -> none  [the longest x1 13.3 us: per_device(): lax.all_gather(key_own, 'ctx', axis=0, tiled=True)]
    ppermute x0 -> x11, starting transfers between devices: none -> 16.3 us  [the longest x10 14.4 us: shift(): return lax.ppermute(a, 'ctx', [p[::-1] for p in pairs] if back else pairs)]
    pallas_call x0 -> x5, Pallas kernels: none -> 16.2 us  [the longest x3 15.5 us: run(): pl.pallas_call(body, in_specs=[pl.BlockSpec(memory_space=pltpu.SMEM)] + [...]
    reduce_sum x1 -> x0, other arithmetic: 9.11 us -> none  [per_device(): jnp.sum(jnp.exp(scores - row_top), axis=2, keepdims=True)]
    ppermute x0 -> x11, waiting for transfers between devices: none -> 7.54 us  [the longest x10 7.54 us: shift(): return lax.ppermute(a, 'ctx', [p[::-1] for p in pairs] if back else pairs)]
    reshape x2 -> x0, local copies, waits for them, and re-layouts: 1.99 us -> none  [the longest x1 1.48 us: per_device(): queries = query_rows.reshape(tokens, q_heads, HEAD_DIM)]
  transfers between devices with their start and end apart: 2 -> 12, of which waited for: 1 -> 3; matrix products, arithmetic and copies ran while one was open for 5% -> 0% of each run, Pallas kernels for 0% -> 29%
where the time goes in v2:
time: 53.5 us; the launch traced here: 52.9 us
  starting transfers between devices  21.8 us (41%)
  Pallas kernels  16.2 us (30%)
  waiting for transfers between devices  7.55 us (14%)
  local copies, waits for them, and re-layouts  5.72 us (11%)
  other arithmetic  0.82 us (2%)
  between operations  0.76 us (1%)
    pallas_call x3, Pallas kernels, run(): pl.pallas_call(body, in_specs=[pl.BlockSpec(memory_space=pltpu.SMEM)] + [...  15.5 us
    ppermute x10, starting transfers between devices, shift(): return lax.ppermute(a, 'ctx', [p[::-1] for p in pairs] if back else pairs)  14.4 us
    ppermute x10, waiting for transfers between devices, shift(): return lax.ppermute(a, 'ctx', [p[::-1] for p in pairs] if back else pairs)  7.54 us
    all_to_all x1, starting transfers between devices, per_device(): lax.all_to_all(owned.reshape(n_head, rows_out, 2 * d), 'head', split_axis...  5.52 us
    unnamed x10, local copies, waits for them, and re-layouts  4.83 us
    ppermute x1, starting transfers between devices, gather(): across = lax.ppermute(far, 'ctx', [(i ^ 1, i) for i in range(n_ctx)])  1.91 us
  transfers between devices with their start and end apart: 12, of which 3 were waited for; matrix products, arithmetic and copies ran while one was open for 0% of the time, Pallas kernels for 29%

profile of v2, /device:TPU:1, one launch (start us, length us, event | category | flops | bytes accessed | tf_op | source)
XLA Modules:
  0.0 52.9 jit_solution(7174515435023518641)
XLA Ops:
  0.6 0.9 %constant_dynamic-slice_fusion = (bf16[256,128]{1,0:T(8,128)(2,1)S(1)}, bf16[256,128]{1,0:T(8,128)(2,1)S(1)}) fusion(bf16[256,1024]{1,0:T(8,128)(2,1)} %param.7, s32[]{:T(128)S(6)} %select_n.10, bf16[256,1024]{1,0:T(8,128)(2,1)} %param.6), kind=kLoop, calls=%fused_computation.9 | loop fusion | bytes 262148 | tf_op jit(solution)/shard_map/dynamic_slice | solution.py:287
  1.6 0.0 copy-start.2
  1.6 0.0 copy-start.3
  1.6 0.0 copy-start.4
  1.6 3.2 %collective-permute-start.1 = (bf16[256,128]{1,0:T(8,128)(2,1)S(1)}, bf16[256,128]{1,0:T(8,128)(2,1)S(1)}, u32[]{:S(2)}, u32[]{:S(2)}) collective-permute-start(bf16[256,128]{1,0:T(8,128)(2,1)S(1)} %get-tuple-element.22.rest_0_), channel_id=1, source_target_pairs={{16,0},{24,8},{0,16},{8,24},{17,1},{25,9},{1,17},{9,25},{18,2},{26... | collective-permute-start | bytes 196616 | tf_op jit(solution)/shard_map/ppermute | solution.py:278
  4.8 1.3 %collective-permute-start = (bf16[256,128]{1,0:T(8,128)(2,1)S(1)}, bf16[256,128]{1,0:T(8,128)(2,1)S(1)}, u32[]{:S(2)}, u32[]{:S(2)}) collective-permute-start(bf16[256,128]{1,0:T(8,128)(2,1)S(1)} %get-tuple-element.22.rest_0_), channel_id=1, source_target_pairs={{8,0},{0,8},{24,16},{16,24},{9,1},{1,9},{25,17},{17,25},{10,2},{2,... | collective-permute-start | bytes 196616 | tf_op jit(solution)/shard_map/ppermute | solution.py:278
  6.1 0.4 collective-permute-done.1.rest_2_
  6.5 1.9 %collective-permute-start.2 = (bf16[256,128]{1,0:T(8,128)(2,1)S(1)}, bf16[256,128]{1,0:T(8,128)(2,1)S(1)}, u32[]{:S(2)}, u32[]{:S(2)}) collective-permute-start(bf16[256,128]{1,0:T(8,128)(2,1)S(1)} %collective-permute-done.1.rest_2_), channel_id=1, source_target_pairs={{8,0},{0,8},{24,16},{16,24},{9,1},{1,9},{25,17},{17,25},{10,2},{2,... | collective-permute-start | bytes 196616 | tf_op jit(solution)/shard_map/ppermute | solution.py:296
  8.4 3.3 %collective-permute-start.5 = (bf16[256,128]{1,0:T(8,128)(2,1)S(1)}, bf16[256,128]{1,0:T(8,128)(2,1)S(1)}, u32[]{:S(2)}, u32[]{:S(2)}) collective-permute-start(bf16[256,128]{1,0:T(8,128)(2,1)S(1)} %get-tuple-element.26.rest_0_), channel_id=1, source_target_pairs={{24,0},{16,8},{8,16},{0,24},{25,1},{17,9},{9,17},{1,25},{26,2},{18... | collective-permute-start | bytes 196616 | tf_op jit(solution)/shard_map/ppermute | solution.py:278
  11.7 0.3 collective-permute-start.4
  12.0 0.3 collective-permute-start.3
  12.3 0.0 collective-permute-done.rest_1_
  12.3 0.0 collective-permute-done.2.rest_3_
  12.3 0.0 copy-done.2
  12.3 0.0 copy-done.3
  12.3 0.0 copy-done.4
  12.3 6.9 %shard_map.84 = (bf16[5,256,2048]{2,1,0:T(8,128)(2,1)S(1)}, f32[2,2048]{1,0:T(2,128)S(1)}, bf16[256,2048]{1,0:T(8,128)(2,1)S(1)}, bf16[1024,128]{1,0:T(8,128)(2,...) custom-call(s32[8]{0:T(128)S(1)} %copy-done.3, ...), custom_call_target="tpu_custom_call" | custom-call | flops 1342177280 | bytes 2621440 | tf_op jit(solution)/shard_map/pallas_call | solution.py:249
  19.2 1.2 %collective-permute-start.9 = (bf16[512,128]{1,0:T(8,128)(2,1)S(1)}, bf16[512,128]{1,0:T(8,128)(2,1)S(1)}, u32[]{:S(2)}, u32[]{:S(2)}) collective-permute-start(bf16[512,128]{1,0:T(8,128)(2,1)S(1)} %pad_maximum_fusion.1), channel_id=1, source_target_pairs={{8,0},{0,8},{24,16},{16,24},{9,1},{1,9},{25,17},{17,25},{10,2},{2,... | collective-permute-start | bytes 393224 | tf_op jit(solution)/shard_map/ppermute | solution.py:278
  20.4 0.0 collective-permute-done.5.rest_3_
  20.4 0.0 collective-permute-done.4.rest_2_
  20.4 0.0 collective-permute-done.3.rest_1_
  20.5 6.0 %shard_map.85 = (bf16[256,2048]{1,0:T(8,128)(2,1)}, bf16[5,256,2048]{2,1,0:T(8,128)(2,1)S(1)}, bf16[256,128]{1,0:T(8,128)(2,1)S(1)}, bf16[256,128]{1,0:T(8,128)(...) custom-call(s32[8]{0:T(128)S(1)} %copy-done.3, bf16[5,256,2048]{2,1,0:T(8,128)(2,1)S(1)} %get-tuple-element.23.p_ref, ...), custom_call_target="tpu_custom_call" | custom-call | flops 2013265920 | bytes 3932160 | tf_op jit(solution)/shard_map/pallas_call | solution.py:249
  26.4 0.0 copy-start
  26.4 2.3 %copy-done = bf16[5,256,2048]{2,1,0:T(8,128)(2,1)} copy-done((bf16[5,256,2048]{2,1,0:T(8,128)(2,1)}, bf16[5,256,2048]{2,1,0:T(8,128)(2,1)S(1)}, u32[]{:S(2)}) %copy-start) | copy-done | bytes 5242904
  28.8 0.3 collective-permute-start.6
  29.0 2.4 %collective-permute-start.7 = (bf16[256,128]{1,0:T(8,128)(2,1)S(1)}, bf16[256,128]{1,0:T(8,128)(2,1)S(1)}, u32[]{:S(2)}, u32[]{:S(2)}) collective-permute-start(bf16[256,128]{1,0:T(8,128)(2,1)S(1)} %get-tuple-element.32), channel_id=1, source_target_pairs={{0,16},{8,24},{16,0},{24,8},{1,17},{9,25},{17,1},{25,9},{2,18},{10... | collective-permute-start | bytes 196616 | tf_op jit(solution)/shard_map/ppermute | solution.py:278
  31.4 0.9 %collective-permute-start.8 = (bf16[256,128]{1,0:T(8,128)(2,1)S(1)}, bf16[256,128]{1,0:T(8,128)(2,1)S(1)}, u32[]{:S(2)}, u32[]{:S(2)}) collective-permute-start(bf16[256,128]{1,0:T(8,128)(2,1)S(1)} %get-tuple-element.33), channel_id=1, source_target_pairs={{0,24},{8,16},{16,8},{24,0},{1,25},{9,17},{17,9},{25,1},{2,26},{10... | collective-permute-start | bytes 196616 | tf_op jit(solution)/shard_map/ppermute | solution.py:278
  32.3 0.0 collective-permute-done.9
  32.4 1.2 %collective-permute-start.10 = (bf16[256,128]{1,0:T(8,128)(2,1)S(1)}, bf16[256,128]{1,0:T(8,128)(2,1)S(1)}, u32[]{:S(2)}, u32[]{:S(2)}) collective-permute-start(bf16[256,128]{1,0:T(8,128)(2,1)S(1)} %fusion), channel_id=1, source_target_pairs={{16,0},{24,8},{0,16},{8,24},{17,1},{25,9},{1,17},{9,25},{18,2},{26... | collective-permute-start | bytes 196616 | tf_op jit(solution)/shard_map/ppermute | solution.py:278
  33.6 0.0 collective-permute-done.6
  33.6 0.0 collective-permute-done.7
  33.6 3.0 %collective-permute-done.8 = bf16[256,128]{1,0:T(8,128)(2,1)S(1)} collective-permute-done((bf16[256,128]{1,0:T(8,128)(2,1)S(1)}, bf16[256,128]{1,0:T(8,128)(2,1)S(1)}, u32[]{:S(2)}, u32[]{:S(2)}) %collective-permute-start.8) | collective-permute-done | bytes 65568 | tf_op jit(solution)/shard_map/ppermute | solution.py:278
  36.7 4.2 %collective-permute-done.10 = bf16[256,128]{1,0:T(8,128)(2,1)S(1)} collective-permute-done((bf16[256,128]{1,0:T(8,128)(2,1)S(1)}, bf16[256,128]{1,0:T(8,128)(2,1)S(1)}, u32[]{:S(2)}, u32[]{:S(2)}) %collective-permute-start.10) | collective-permute-done | bytes 65568 | tf_op jit(solution)/shard_map/ppermute | solution.py:278
  40.9 0.7 %pad_maximum_fusion.2 = bf16[256,256]{1,0:T(8,128)(2,1)} fusion(bf16[256,128]{1,0:T(8,128)(2,1)S(1)} %fusion.2, bf16[256,128]{1,0:T(8,128)(2,1)S(1)} %add_convert_fusion), kind=kLoop, calls=%fused_computation.7 | loop fusion | flops 262144 | bytes 262144 | tf_op jit(solution)/shard_map/concatenate | solution.py:335
  41.5 5.5 %all-to-all-start = ((bf16[8,32,256]{2,1,0:T(8,128)(2,1)}), bf16[8,32,256]{2,1,0:T(8,128)(2,1)S(1)}, u32[]{:S(2)}, u32[]{:S(2)}) async-start(bf16[8,32,256]{2,1,0:T(8,128)(2,1)} %bitcast), calls=%async_computation | async-start | bytes 262144 | tf_op jit(solution)/shard_map/all_to_all | solution.py:336
  47.1 0.0 copy-start.1
  47.1 2.5 %copy-done.1 = bf16[5,256,2048]{2,1,0:T(8,128)(2,1)S(1)} copy-done((bf16[5,256,2048]{2,1,0:T(8,128)(2,1)S(1)}, bf16[5,256,2048]{2,1,0:T(8,128)(2,1)}, u32[]{:S(2)}) %copy-start.1) | copy-done | bytes 5242904
  49.5 2.7 %shard_map.86 = bf16[256,2048]{1,0:T(8,128)(2,1)} custom-call(s32[8]{0:T(128)S(1)} %copy-done.3, bf16[5,256,2048]{2,1,0:T(8,128)(2,1)S(1)} %copy-done.1, bf16[1024,128]{1,0:T(8,128)(2,1)S(1)} %get-tuple-element.29.k_ref), custom_call_target="tpu_custom_call" | custom-call | flops 671088640 | bytes 1310720 | tf_op jit(solution)/shard_map/pallas_call | solution.py:249
  52.2 0.0 all-to-all-done
  52.2 0.7 %total.1 = (bf16[32,1024]{1,0:T(8,128)(2,1)}, bf16[32,1024]{1,0:T(8,128)(2,1)}) custom-call(bf16[8,1,32,256]{3,2,1,0:T(8,128)(2,1)S(1)} %bitcast.2), custom_call_target="tpu_custom_call" | custom-call | tf_op jit(solution)/shard_map/total/pallas_call | solution.py:355
  (7 shorter events, 0.1 us)
Async XLA Ops:
  1.6 10.7 %copy-start.2 = (bf16[256,2048]{1,0:T(8,128)(2,1)S(1)}, bf16[256,2048]{1,0:T(8,128)(2,1)}, u32[]{:S(2)}) copy-start(bf16[256,2048]{1,0:T(8,128)(2,1)} %q_ref.3) | copy-start | bytes 3145732
  1.6 10.7 %copy-start.3 = (s32[8]{0:T(128)S(1)}, s32[8]{0:T(128)}, u32[]{:S(2)}) copy-start(s32[8]{0:T(128)} %meta.5) | copy-start | bytes 100
  1.6 10.7 %copy-start.4 = (bf16[256,2048]{1,0:T(8,128)(2,1)S(1)}, bf16[256,2048]{1,0:T(8,128)(2,1)}, u32[]{:S(2)}) copy-start(bf16[256,2048]{1,0:T(8,128)(2,1)} %g_ref.1) | copy-start | bytes 3145732
  1.6 4.8 %collective-permute-start.1 = (bf16[256,128]{1,0:T(8,128)(2,1)S(1)}, bf16[256,128]{1,0:T(8,128)(2,1)S(1)}, u32[]{:S(2)}, u32[]{:S(2)}) collective-permute-start(bf16[256,128]{1,0:T(8,128)(2,1)S(1)} %get-tuple-element.22.rest_0_), channel_id=1, source_target_pairs={{16,0},{24,8},{0,16},{8,24},{17,1},{25,9},{1,17},{9,25},{18,2},{26... | collective-permute-start | bytes 196616 | tf_op jit(solution)/shard_map/ppermute | solution.py:278
  4.8 7.5 %collective-permute-start = (bf16[256,128]{1,0:T(8,128)(2,1)S(1)}, bf16[256,128]{1,0:T(8,128)(2,1)S(1)}, u32[]{:S(2)}, u32[]{:S(2)}) collective-permute-start(bf16[256,128]{1,0:T(8,128)(2,1)S(1)} %get-tuple-element.22.rest_0_), channel_id=1, source_target_pairs={{8,0},{0,8},{24,16},{16,24},{9,1},{1,9},{25,17},{17,25},{10,2},{2,... | collective-permute-start | bytes 196616 | tf_op jit(solution)/shard_map/ppermute | solution.py:278
  6.5 5.8 %collective-permute-start.2 = (bf16[256,128]{1,0:T(8,128)(2,1)S(1)}, bf16[256,128]{1,0:T(8,128)(2,1)S(1)}, u32[]{:S(2)}, u32[]{:S(2)}) collective-permute-start(bf16[256,128]{1,0:T(8,128)(2,1)S(1)} %collective-permute-done.1.rest_2_), channel_id=1, source_target_pairs={{8,0},{0,8},{24,16},{16,24},{9,1},{1,9},{25,17},{17,25},{10,2},{2,... | collective-permute-start | bytes 196616 | tf_op jit(solution)/shard_map/ppermute | solution.py:296
  8.4 12.1 %collective-permute-start.5 = (bf16[256,128]{1,0:T(8,128)(2,1)S(1)}, bf16[256,128]{1,0:T(8,128)(2,1)S(1)}, u32[]{:S(2)}, u32[]{:S(2)}) collective-permute-start(bf16[256,128]{1,0:T(8,128)(2,1)S(1)} %get-tuple-element.26.rest_0_), channel_id=1, source_target_pairs={{24,0},{16,8},{8,16},{0,24},{25,1},{17,9},{9,17},{1,25},{26,2},{18... | collective-permute-start | bytes 196616 | tf_op jit(solution)/shard_map/ppermute | solution.py:278
  11.7 8.8 %collective-permute-start.4 = (bf16[256,128]{1,0:T(8,128)(2,1)S(1)}, bf16[256,128]{1,0:T(8,128)(2,1)S(1)}, u32[]{:S(2)}, u32[]{:S(2)}) collective-permute-start(bf16[256,128]{1,0:T(8,128)(2,1)S(1)} %get-tuple-element.26.rest_0_), channel_id=1, source_target_pairs={{16,0},{24,8},{0,16},{8,24},{17,1},{25,9},{1,17},{9,25},{18,2},{26... | collective-permute-start | bytes 196616 | tf_op jit(solution)/shard_map/ppermute | solution.py:278
  12.0 8.5 %collective-permute-start.3 = (bf16[256,128]{1,0:T(8,128)(2,1)S(1)}, bf16[256,128]{1,0:T(8,128)(2,1)S(1)}, u32[]{:S(2)}, u32[]{:S(2)}) collective-permute-start(bf16[256,128]{1,0:T(8,128)(2,1)S(1)} %get-tuple-element.26.rest_0_), channel_id=1, source_target_pairs={{8,0},{0,8},{24,16},{16,24},{9,1},{1,9},{25,17},{17,25},{10,2},{2,... | collective-permute-start | bytes 196616 | tf_op jit(solution)/shard_map/ppermute | solution.py:278
  19.2 13.1 %collective-permute-start.9 = (bf16[512,128]{1,0:T(8,128)(2,1)S(1)}, bf16[512,128]{1,0:T(8,128)(2,1)S(1)}, u32[]{:S(2)}, u32[]{:S(2)}) collective-permute-start(bf16[512,128]{1,0:T(8,128)(2,1)S(1)} %pad_maximum_fusion.1), channel_id=1, source_target_pairs={{8,0},{0,8},{24,16},{16,24},{9,1},{1,9},{25,17},{17,25},{10,2},{2,... | collective-permute-start | bytes 393224 | tf_op jit(solution)/shard_map/ppermute | solution.py:278
  26.4 2.3 %copy-start = (bf16[5,256,2048]{2,1,0:T(8,128)(2,1)}, bf16[5,256,2048]{2,1,0:T(8,128)(2,1)S(1)}, u32[]{:S(2)}) copy-start(bf16[5,256,2048]{2,1,0:T(8,128)(2,1)S(1)} %get-tuple-element.28.ds_ref) | copy-start | bytes 15728644
  28.8 4.9 %collective-permute-start.6 = (bf16[256,128]{1,0:T(8,128)(2,1)S(1)}, bf16[256,128]{1,0:T(8,128)(2,1)S(1)}, u32[]{:S(2)}, u32[]{:S(2)}) collective-permute-start(bf16[256,128]{1,0:T(8,128)(2,1)S(1)} %get-tuple-element.31), channel_id=1, source_target_pairs={{0,8},{8,0},{16,24},{24,16},{1,9},{9,1},{17,25},{25,17},{2,10},{10... | collective-permute-start | bytes 196616 | tf_op jit(solution)/shard_map/ppermute | solution.py:278
  29.0 4.6 %collective-permute-start.7 = (bf16[256,128]{1,0:T(8,128)(2,1)S(1)}, bf16[256,128]{1,0:T(8,128)(2,1)S(1)}, u32[]{:S(2)}, u32[]{:S(2)}) collective-permute-start(bf16[256,128]{1,0:T(8,128)(2,1)S(1)} %get-tuple-element.32), channel_id=1, source_target_pairs={{0,16},{8,24},{16,0},{24,8},{1,17},{9,25},{17,1},{25,9},{2,18},{10... | collective-permute-start | bytes 196616 | tf_op jit(solution)/shard_map/ppermute | solution.py:278
  31.4 5.2 %collective-permute-start.8 = (bf16[256,128]{1,0:T(8,128)(2,1)S(1)}, bf16[256,128]{1,0:T(8,128)(2,1)S(1)}, u32[]{:S(2)}, u32[]{:S(2)}) collective-permute-start(bf16[256,128]{1,0:T(8,128)(2,1)S(1)} %get-tuple-element.33), channel_id=1, source_target_pairs={{0,24},{8,16},{16,8},{24,0},{1,25},{9,17},{17,9},{25,1},{2,26},{10... | collective-permute-start | bytes 196616 | tf_op jit(solution)/shard_map/ppermute | solution.py:278
  32.4 8.5 %collective-permute-start.10 = (bf16[256,128]{1,0:T(8,128)(2,1)S(1)}, bf16[256,128]{1,0:T(8,128)(2,1)S(1)}, u32[]{:S(2)}, u32[]{:S(2)}) collective-permute-start(bf16[256,128]{1,0:T(8,128)(2,1)S(1)} %fusion), channel_id=1, source_target_pairs={{16,0},{24,8},{0,16},{8,24},{17,1},{25,9},{1,17},{9,25},{18,2},{26... | collective-permute-start | bytes 196616 | tf_op jit(solution)/shard_map/ppermute | solution.py:278
  41.5 10.7 %all-to-all-start = ((bf16[8,32,256]{2,1,0:T(8,128)(2,1)}), bf16[8,32,256]{2,1,0:T(8,128)(2,1)S(1)}, u32[]{:S(2)}, u32[]{:S(2)}) async-start(bf16[8,32,256]{2,1,0:T(8,128)(2,1)} %bitcast), calls=%async_computation | async-start | bytes 262144 | tf_op jit(solution)/shard_map/all_to_all | solution.py:336
  47.1 2.5 %copy-start.1 = (bf16[5,256,2048]{2,1,0:T(8,128)(2,1)S(1)}, bf16[5,256,2048]{2,1,0:T(8,128)(2,1)}, u32[]{:S(2)}) copy-start(bf16[5,256,2048]{2,1,0:T(8,128)(2,1)} %copy-done) | copy-start | bytes 15728644

commit v3 on v2

--- a/solution.py
+++ b/solution.py
@@ -35,16 +35,24 @@
 
 class Plan:
     def __init__(self, n_ctx, span, meta):
-        self.n_ctx, self.span, self.meta = n_ctx, span, meta
+        self.n_ctx, self.span = n_ctx, span
         self.tile = 2 * span
         self.slots = n_ctx + 1
         self.ctx = lax.axis_index("ctx")
-        first, second = meta[2 * self.ctx], meta[2 * self.ctx + 1]
+        table = meta[...]
+        self.order = [table[0, i] for i in range(2 * n_ctx)]
+        first, second = self.position(self.ctx, 0), self.position(self.ctx, 1)
         self.hi, self.lo = jnp.maximum(first, second), jnp.minimum(first, second)
         hi_row = pl.multiple_of(jnp.where(first > second, 0, span), span)
         self.row = {True: hi_row, False: pl.multiple_of(span - hi_row, span)}
         self.hi_tiles = (self.hi + 2) // 2
         self.sure_hi = (n_ctx + 2) // 2
+
+    def position(self, ctx, half):
+        out = self.order[half]
+        for c in range(1, self.n_ctx):
+            out = jnp.where(ctx == c, self.order[2 * c + half], out)
+        return out
 
     def kind(self, t):
         if t < self.sure_hi:
@@ -86,7 +94,7 @@
         for r, shard in enumerate(shards):
             src = partner(self.ctx, r, self.n_ctx)
             for half in range(2):
-                pos = self.meta[2 * src + half]
+                pos = self.position(src, half)
                 rows = pl.ds(pl.multiple_of(pos * self.span, self.span), self.span)
                 out[rows, :] = shard[half * self.span : (half + 1) * self.span, :]
 
@@ -94,7 +102,7 @@
         for r, out in enumerate(outs):
             dest = partner(self.ctx, r, self.n_ctx)
             for half in range(2):
-                pos = self.meta[2 * dest + half]
+                pos = self.position(dest, half)
                 rows = pl.ds(pl.multiple_of(pos * self.span, self.span), self.span)
                 out[half * self.span : (half + 1) * self.span, :] = total(rows)
 
@@ -117,6 +125,18 @@
             else:
                 out.append(pair[self.kind(t)])
         return pair, out
+
+
+def pipeline(stages, parts):
+    states = [{} for _ in parts]
+    for step in range(len(parts) + len(stages) - 1):
+        running = [
+            stage(parts[step - k], states[step - k])
+            for k, stage in reversed(list(enumerate(stages)))
+            if 0 <= step - k < len(parts)
+        ]
+        while running:
+            running = [r for r in running if next(r, running) is not running]
 
 
 def groups(width, heads):
@@ -157,9 +177,10 @@
     diff = lax.broadcasted_iota(jnp.int32, (plan.tile, width), 0) - lax.rem(
         lax.broadcasted_iota(jnp.int32, (plan.tile, width), 1), span
     )
-    for cols in groups(q_ref.shape[1], heads):
+
+    def score(cols, state):
+        state["tops"] = tops = {True: None, False: None}
         _, qs = plan.slot_queries(q_ref, cols)
-        tops = {True: None, False: None}
         for t in range(plan.slots):
             s = dot_nt(k_ref[plan.keys(t), :], qs[t])
             if t >= plan.sure_hi - 1:
@@ -168,11 +189,16 @@
                 s = jnp.where(diff <= limit, s, -jnp.inf)
             s_ref[t, :, cols] = s
             plan.fold(tops, t, jnp.max(s, axis=0, keepdims=True), jnp.maximum, -jnp.inf)
+            yield
+
+    def exponent(cols, state):
+        tops = state["tops"]
         sums = {True: None, False: None}
         for t in range(plan.slots):
             p = jnp.exp2((s_ref[t, :, cols] - plan.pick(t, tops)) * EXP_SCALE)
             p_ref[t, :, cols] = p.astype(BF16)
             plan.fold(sums, t, jnp.sum(p, axis=0, keepdims=True), jnp.add, 0.0)
+            yield
         for kind, r in ((True, 0), (False, 1)):
             inverse = 1.0 / sums[kind]
             inv_ref[r : r + 1, cols] = inverse
@@ -182,9 +208,14 @@
                 column = jnp.broadcast_to(row, (span, span)).T
                 g = g_ref[pl.ds(plan.row[kind], span), here].astype(F32)
                 gs_ref[pl.ds(plan.row[kind], span), here] = (g * column).astype(BF16)
+
+    def value(cols, state):
         _, gs = plan.slot_queries(gs_ref, cols)
         for t in range(plan.slots):
             acc_ref[plan.keys(t), :] += dot_nn(p_ref[t, :, cols], gs[t])
+            yield
+
+    pipeline((score, exponent, value), groups(q_ref.shape[1], heads))
     plan.unsort(lambda rows: acc_ref[rows, :].astype(BF16), dv_refs)
 
 
@@ -199,14 +230,14 @@
     for t in range(n_ctx):
         vt_ref[t] = v_ref[t * plan.tile : (t + 1) * plan.tile, :].astype(F32).T.astype(BF16)
     acc_ref[...] = jnp.zeros_like(acc_ref)
-    for cols in groups(q_ref.shape[1], heads):
-        _, qs = plan.slot_queries(q_ref, cols)
-        _, gs = plan.slot_queries(gs_ref, cols)
+
+    def output(cols, state):
         outs = {True: None, False: None}
         for t in range(plan.slots):
             part = dot_nn(vt_ref[plan.key_tile(t)], p_ref[t, :, cols])
             plan.fold(outs, t, part, jnp.add, 0.0)
-        dots = {}
+            yield
+        state["dots"] = dots = {}
         for kind, r in ((True, 0), (False, 1)):
             out = outs[kind] * inv_ref[r : r + 1, cols]
             parts = []
@@ -217,11 +248,19 @@
                 g = gs_ref[pl.ds(plan.row[kind], span), here].astype(F32)
                 parts.append(jnp.sum((g * o.astype(F32)).T, axis=0, keepdims=True))
             dots[kind] = jnp.concatenate(parts, axis=1)
+
+    def score_grad(cols, state):
+        _, qs = plan.slot_queries(q_ref, cols)
+        _, gs = plan.slot_queries(gs_ref, cols)
         for t in range(plan.slots):
             dp = dot_nt(v_ref[plan.keys(t), :], gs[t])
-            ds = (p_ref[t, :, cols].astype(F32) * (dp - plan.pick(t, dots))).astype(BF16)
+            dots = plan.pick(t, state["dots"])
+            ds = (p_ref[t, :, cols].astype(F32) * (dp - dots)).astype(BF16)
             ds_ref[t, :, cols] = ds
             acc_ref[plan.keys(t), :] += dot_nn(ds, qs[t])
+            yield
+
+    pipeline((output, score_grad), groups(q_ref.shape[1], heads))
     plan.unsort(lambda rows: (acc_ref[rows, :] * SCALE).astype(BF16), dk_refs)
 
 
@@ -248,7 +287,7 @@
     def run(meta, *args):
         return pl.pallas_call(
             body,
-            in_specs=[pl.BlockSpec(memory_space=pltpu.SMEM)] + [vmem] * len(args),
+            in_specs=[vmem] * (1 + len(args)),
             out_specs=[vmem] * len(out_shape),
             out_shape=out_shape,
             scratch_shapes=scratch,
@@ -281,6 +320,7 @@
         return jax.ShapeDtypeStruct(dims, dtype)
 
     others = range(1, n_ctx)
+    order = span_order.reshape(1, 2 * n_ctx)
     kv_group = lax.axis_index("head") * q_heads // GROUP
     own = lax.optimization_barrier(
         jnp.concatenate(
@@ -305,7 +345,7 @@
         bind(forward_kernel),
         [shape(slots), pair, rows, shape((keys, d))] + [shard] * n_ctx,
         [pltpu.VMEM(slots, F32), pltpu.VMEM((keys, d), F32)], 2 * work,
-    )(span_order, query_rows, out_grad, *key_shards)
+    )(order, query_rows, out_grad, *key_shards)
     attn_out, score_grads, *key_parts = call(
         bind(backward_kernel), [rows, shape(slots)] + [shard] * n_ctx,
         [
@@ -313,25 +353,27 @@
             pltpu.VMEM((n_ctx, d, tokens), BF16),
             pltpu.VMEM((keys, d), F32),
         ], 3 * work,
-    )(span_order, p, inverse, grads, query_rows, *value_shards)
+    )(order, p, inverse, grads, query_rows, *value_shards)
     (query_grad,) = call(
         bind(query_kernel), [rows],
         [pltpu.VMEM((n_ctx, d, tokens), BF16)], work,
-    )(span_order, score_grads, key_sorted)
-
-    def scatter(parts, name):
-        if n_ctx == 4 and name == "value_grad":
-            given = jnp.concatenate([parts[1], parts[3]])
-            taken = shift(given, 1).astype(F32)
-            far = (parts[2].astype(F32) + taken[tokens:]).astype(BF16)
-            far = shift(far, 2).astype(F32)
-            return (parts[0].astype(F32) + taken[:tokens] + far).astype(BF16)
-        total = parts[0].astype(F32)
-        for r in others:
-            total += shift(parts[r], r, True).astype(F32)
-        return total.astype(BF16)
-
-    value_sum, key_sum = scatter(value_parts, "value_grad"), scatter(key_parts, "key_grad")
+    )(order, score_grads, key_sorted)
+
+    def plus(*parts):
+        return functools.reduce(jnp.add, [a.astype(F32) for a in parts])
+
+    if n_ctx == 4:
+        far = shift(jnp.concatenate(value_parts[2:]), 2)
+        near = plus(value_parts[1], far[tokens:]).astype(BF16)
+        near = shift(jnp.concatenate([near, key_parts[1]]), 1)
+        value_sum = plus(value_parts[0], far[:tokens], near[:tokens])
+        key_sum = plus(key_parts[0], near[tokens:], *[shift(key_parts[r], r) for r in (2, 3)])
+    else:
+        value_sum, key_sum = [
+            plus(parts[0], *[shift(parts[r], r, True) for r in others])
+            for parts in (value_parts, key_parts)
+        ]
+    key_sum, value_sum = key_sum.astype(BF16), value_sum.astype(BF16)
     owned = jnp.concatenate([key_sum, value_sum], axis=1)
     parts = lax.all_to_all(
         owned.reshape(n_head, rows_out, 2 * d), "head", split_axis=0, concat_axis=0

time: 53.5 us -> 50.2 us (0.938)
  the two profiles are of different devices: /device:TPU:1 before, /device:TPU:0 now
where the time goes in v3:
time: 50.2 us; the launch traced here: 49.9 us
  starting transfers between devices  22 us (44%)
  Pallas kernels  14.6 us (29%)
  waiting for transfers between devices  5.97 us (12%)
  local copies, waits for them, and re-layouts  5.72 us (11%)
  other arithmetic  0.82 us (2%)
  between operations  0.77 us (2%)
    ppermute x9, starting transfers between devices, shift(): return lax.ppermute(a, 'ctx', [p[::-1] for p in pairs] if back else pairs)  16.9 us
    pallas_call x3, Pallas kernels, run(): pl.pallas_call(body, in_specs=[vmem] * (1 + len(args)), out_specs=[vmem]...  13.9 us
    ppermute x9, waiting for transfers between devices, shift(): return lax.ppermute(a, 'ctx', [p[::-1] for p in pairs] if back else pairs)  5.13 us
    unnamed x10, local copies, waits for them, and re-layouts  4.83 us
    all_to_all x1, starting transfers between devices, per_device(): lax.all_to_all(owned.reshape(n_head, rows_out, 2 * d), 'head', split_axis...  3.75 us
    ppermute x1, starting transfers between devices, gather(): across = lax.ppermute(far, 'ctx', [(i ^ 1, i) for i in range(n_ctx)])  1.37 us
  transfers between devices with their start and end apart: 11, of which 3 were waited for; matrix products, arithmetic and copies ran while one was open for 0% of the time, Pallas kernels for 28%

profile of v3, /device:TPU:0, one launch (start us, length us, event | category | flops | bytes accessed | tf_op | source)
XLA Modules:
  0.0 49.9 jit_solution(12765499089072664716)
XLA Ops:
  0.6 0.9 %constant_dynamic-slice_fusion = (bf16[256,128]{1,0:T(8,128)(2,1)S(1)}, bf16[256,128]{1,0:T(8,128)(2,1)S(1)}) fusion(bf16[256,1024]{1,0:T(8,128)(2,1)} %param.7, s32[]{:T(128)S(6)} %select_n.10, bf16[256,1024]{1,0:T(8,128)(2,1)} %param.6), kind=kLoop, calls=%fused_computation.7 | loop fusion | bytes 262148 | tf_op jit(solution)/shard_map/dynamic_slice | solution.py:327
  1.6 0.0 copy-start.2
  1.6 0.0 copy-start.3
  1.6 0.0 copy-start.4
  1.6 4.1 %collective-permute-start.1 = (bf16[256,128]{1,0:T(8,128)(2,1)S(1)}, bf16[256,128]{1,0:T(8,128)(2,1)S(1)}, u32[]{:S(2)}, u32[]{:S(2)}) collective-permute-start(bf16[256,128]{1,0:T(8,128)(2,1)S(1)} %get-tuple-element.22.rest_0_), channel_id=1, source_target_pairs={{16,0},{24,8},{0,16},{8,24},{17,1},{25,9},{1,17},{9,25},{18,2},{26... | collective-permute-start | bytes 196616 | tf_op jit(solution)/shard_map/ppermute | solution.py:317
  5.7 1.6 %collective-permute-start = (bf16[256,128]{1,0:T(8,128)(2,1)S(1)}, bf16[256,128]{1,0:T(8,128)(2,1)S(1)}, u32[]{:S(2)}, u32[]{:S(2)}) collective-permute-start(bf16[256,128]{1,0:T(8,128)(2,1)S(1)} %get-tuple-element.22.rest_0_), channel_id=1, source_target_pairs={{8,0},{0,8},{24,16},{16,24},{9,1},{1,9},{25,17},{17,25},{10,2},{2,... | collective-permute-start | bytes 196616 | tf_op jit(solution)/shard_map/ppermute | solution.py:317
  7.3 1.5 %collective-permute-done.1.rest_2_ = bf16[256,128]{1,0:T(8,128)(2,1)S(1)} collective-permute-done((bf16[256,128]{1,0:T(8,128)(2,1)S(1)}, bf16[256,128]{1,0:T(8,128)(2,1)S(1)}, u32[]{:S(2)}, u32[]{:S(2)}) %collective-permute-start.1) | collective-permute-done | bytes 65568 | tf_op jit(solution)/shard_map/ppermute | solution.py:317
  8.8 1.4 %collective-permute-start.2 = (bf16[256,128]{1,0:T(8,128)(2,1)S(1)}, bf16[256,128]{1,0:T(8,128)(2,1)S(1)}, u32[]{:S(2)}, u32[]{:S(2)}) collective-permute-start(bf16[256,128]{1,0:T(8,128)(2,1)S(1)} %collective-permute-done.1.rest_2_), channel_id=1, source_target_pairs={{8,0},{0,8},{24,16},{16,24},{9,1},{1,9},{25,17},{17,25},{10,2},{2,... | collective-permute-start | bytes 196616 | tf_op jit(solution)/shard_map/ppermute | solution.py:336
  10.2 2.7 %collective-permute-start.5 = (bf16[256,128]{1,0:T(8,128)(2,1)S(1)}, bf16[256,128]{1,0:T(8,128)(2,1)S(1)}, u32[]{:S(2)}, u32[]{:S(2)}) collective-permute-start(bf16[256,128]{1,0:T(8,128)(2,1)S(1)} %get-tuple-element.26.rest_0_), channel_id=1, source_target_pairs={{24,0},{16,8},{8,16},{0,24},{25,1},{17,9},{9,17},{1,25},{26,2},{18... | collective-permute-start | bytes 196616 | tf_op jit(solution)/shard_map/ppermute | solution.py:317
  12.9 0.4 collective-permute-start.4
  13.3 1.2 %collective-permute-start.3 = (bf16[256,128]{1,0:T(8,128)(2,1)S(1)}, bf16[256,128]{1,0:T(8,128)(2,1)S(1)}, u32[]{:S(2)}, u32[]{:S(2)}) collective-permute-start(bf16[256,128]{1,0:T(8,128)(2,1)S(1)} %get-tuple-element.26.rest_0_), channel_id=1, source_target_pairs={{8,0},{0,8},{24,16},{16,24},{9,1},{1,9},{25,17},{17,25},{10,2},{2,... | collective-permute-start | bytes 196616 | tf_op jit(solution)/shard_map/ppermute | solution.py:317
  14.6 0.0 collective-permute-done.rest_1_
  14.6 0.0 collective-permute-done.2.rest_3_
  14.6 0.0 copy-done.2
  14.6 0.0 copy-done.3
  14.6 0.0 copy-done.4
  14.6 6.2 %shard_map.84 = (bf16[5,256,2048]{2,1,0:T(8,128)(2,1)S(1)}, f32[2,2048]{1,0:T(2,128)S(1)}, bf16[256,2048]{1,0:T(8,128)(2,1)S(1)}, bf16[1024,128]{1,0:T(8,128)(2,...) custom-call(s32[1,8]{1,0:T(1,128)S(1)} %bitcast.4, ...), custom_call_target="tpu_custom_call" | custom-call | flops 1342177280 | bytes 2621440 | tf_op jit(solution)/shard_map/pallas_call | solution.py:288
  20.8 2.3 %collective-permute-start.6 = (bf16[512,128]{1,0:T(8,128)(2,1)S(1)}, bf16[512,128]{1,0:T(8,128)(2,1)S(1)}, u32[]{:S(2)}, u32[]{:S(2)}) collective-permute-start(bf16[512,128]{1,0:T(8,128)(2,1)S(1)} %pad_maximum_fusion.1), channel_id=1, source_target_pairs={{16,0},{24,8},{0,16},{8,24},{17,1},{25,9},{1,17},{9,25},{18,2},{26... | collective-permute-start | bytes 393224 | tf_op jit(solution)/shard_map/ppermute | solution.py:317
  23.2 0.0 collective-permute-done.5.rest_3_
  23.2 0.0 collective-permute-done.4.rest_2_
  23.2 0.0 collective-permute-done.3.rest_1_
  23.2 5.6 %shard_map.85 = (bf16[256,2048]{1,0:T(8,128)(2,1)}, bf16[5,256,2048]{2,1,0:T(8,128)(2,1)S(1)}, bf16[256,128]{1,0:T(8,128)(2,1)S(1)}, bf16[256,128]{1,0:T(8,128)(...) custom-call(s32[1,8]{1,0:T(1,128)S(1)} %bitcast.5, ...), custom_call_target="tpu_custom_call" | custom-call | flops 2013265920 | bytes 3932160 | tf_op jit(solution)/shard_map/pallas_call | solution.py:288
  28.7 0.0 copy-start
  28.7 2.3 %copy-done = bf16[5,256,2048]{2,1,0:T(8,128)(2,1)} copy-done((bf16[5,256,2048]{2,1,0:T(8,128)(2,1)}, bf16[5,256,2048]{2,1,0:T(8,128)(2,1)S(1)}, u32[]{:S(2)}) %copy-start) | copy-done | bytes 5242904
  31.1 0.0 collective-permute-done.6
  31.1 1.6 %collective-permute-start.7 = (bf16[512,128]{1,0:T(8,128)(2,1)S(1)}, bf16[512,128]{1,0:T(8,128)(2,1)S(1)}, u32[]{:S(2)}, u32[]{:S(2)}) collective-permute-start(bf16[512,128]{1,0:T(8,128)(2,1)S(1)} %pad_maximum_fusion.2), channel_id=1, source_target_pairs={{8,0},{0,8},{24,16},{16,24},{9,1},{1,9},{25,17},{17,25},{10,2},{2,... | collective-permute-start | bytes 393224 | tf_op jit(solution)/shard_map/ppermute | solution.py:317
  32.7 0.0 collective-permute-start.8
  32.8 2.8 %collective-permute-start.9 = (bf16[256,128]{1,0:T(8,128)(2,1)S(1)}, bf16[256,128]{1,0:T(8,128)(2,1)S(1)}, u32[]{:S(2)}, u32[]{:S(2)}) collective-permute-start(bf16[256,128]{1,0:T(8,128)(2,1)S(1)} %get-tuple-element.36), channel_id=1, source_target_pairs={{24,0},{16,8},{8,16},{0,24},{25,1},{17,9},{9,17},{1,25},{26,2},{18... | collective-permute-start | bytes 196616 | tf_op jit(solution)/shard_map/ppermute | solution.py:317
  35.6 3.6 %collective-permute-done.8 = bf16[256,128]{1,0:T(8,128)(2,1)S(1)} collective-permute-done((bf16[256,128]{1,0:T(8,128)(2,1)S(1)}, bf16[256,128]{1,0:T(8,128)(2,1)S(1)}, u32[]{:S(2)}, u32[]{:S(2)}) %collective-permute-start.8) | collective-permute-done | bytes 65568 | tf_op jit(solution)/shard_map/ppermute | solution.py:317
  39.2 0.0 collective-permute-done.9
  39.2 0.0 collective-permute-done.7
  39.2 0.1 add_convert_fusion.1
  39.3 0.7 %pad_maximum_fusion.3 = bf16[256,256]{1,0:T(8,128)(2,1)} fusion(bf16[256,128]{1,0:T(8,128)(2,1)S(1)} %get-tuple-element.41, bf16[256,128]{1,0:T(8,128)(2,1)S(1)} %get-tuple-element.40), kind=kLoop, calls=%fused_computation.3 | loop fusion | flops 262144 | bytes 262144 | tf_op jit(solution)/shard_map/concatenate | solution.py:377
  40.0 3.7 %all-to-all-start = ((bf16[8,32,256]{2,1,0:T(8,128)(2,1)}), bf16[8,32,256]{2,1,0:T(8,128)(2,1)S(1)}, u32[]{:S(2)}, u32[]{:S(2)}) async-start(bf16[8,32,256]{2,1,0:T(8,128)(2,1)} %bitcast.1), calls=%async_computation | async-start | bytes 262144 | tf_op jit(solution)/shard_map/all_to_all | solution.py:378
  43.7 0.0 copy-start.1
  43.7 2.5 %copy-done.1 = bf16[5,256,2048]{2,1,0:T(8,128)(2,1)S(1)} copy-done((bf16[5,256,2048]{2,1,0:T(8,128)(2,1)S(1)}, bf16[5,256,2048]{2,1,0:T(8,128)(2,1)}, u32[]{:S(2)}) %copy-start.1) | copy-done | bytes 5242904
  46.2 2.2 %shard_map.86 = bf16[256,2048]{1,0:T(8,128)(2,1)} custom-call(s32[1,8]{1,0:T(1,128)S(1)} %bitcast.6, bf16[5,256,2048]{2,1,0:T(8,128)(2,1)S(1)} %copy-done.1, bf16[1024,128]{1,0:T(8,128)(2,1)S(1)} %get-tuple-element.29.k_ref), custom_call_target="tpu_custom_call" | custom-call | flops 671088640 | bytes 1310720 | tf_op jit(solution)/shard_map/pallas_call | solution.py:288
  48.4 0.8 %all-to-all-done = bf16[8,32,256]{2,1,0:T(8,128)(2,1)S(1)} async-done(((bf16[8,32,256]{2,1,0:T(8,128)(2,1)}), bf16[8,32,256]{2,1,0:T(8,128)(2,1)S(1)}, u32[]{:S(2)}, u32[]{:S(2)}) %all-to-all-start) | async-done | bytes 131104 | tf_op jit(solution)/shard_map/all_to_all | solution.py:378
  49.2 0.7 %total.1 = (bf16[32,1024]{1,0:T(8,128)(2,1)}, bf16[32,1024]{1,0:T(8,128)(2,1)}) custom-call(bf16[8,1,32,256]{3,2,1,0:T(8,128)(2,1)S(1)} %bitcast.3), custom_call_target="tpu_custom_call" | custom-call | tf_op jit(solution)/shard_map/total/pallas_call | solution.py:397
  (5 shorter events, 0.1 us)
Async XLA Ops:
  1.6 13.0 %copy-start.2 = (bf16[256,2048]{1,0:T(8,128)(2,1)S(1)}, bf16[256,2048]{1,0:T(8,128)(2,1)}, u32[]{:S(2)}) copy-start(bf16[256,2048]{1,0:T(8,128)(2,1)} %q_ref.3) | copy-start | bytes 3145732
  1.6 13.0 %copy-start.3 = (s32[8]{0:T(128)S(1)}, s32[8]{0:T(128)}, u32[]{:S(2)}) copy-start(s32[8]{0:T(128)} %param.9) | copy-start | bytes 100
  1.6 13.0 %copy-start.4 = (bf16[256,2048]{1,0:T(8,128)(2,1)S(1)}, bf16[256,2048]{1,0:T(8,128)(2,1)}, u32[]{:S(2)}) copy-start(bf16[256,2048]{1,0:T(8,128)(2,1)} %g_ref.1) | copy-start | bytes 3145732
  1.6 7.2 %collective-permute-start.1 = (bf16[256,128]{1,0:T(8,128)(2,1)S(1)}, bf16[256,128]{1,0:T(8,128)(2,1)S(1)}, u32[]{:S(2)}, u32[]{:S(2)}) collective-permute-start(bf16[256,128]{1,0:T(8,128)(2,1)S(1)} %get-tuple-element.22.rest_0_), channel_id=1, source_target_pairs={{16,0},{24,8},{0,16},{8,24},{17,1},{25,9},{1,17},{9,25},{18,2},{26... | collective-permute-start | bytes 196616 | tf_op jit(solution)/shard_map/ppermute | solution.py:317
  5.7 8.8 %collective-permute-start = (bf16[256,128]{1,0:T(8,128)(2,1)S(1)}, bf16[256,128]{1,0:T(8,128)(2,1)S(1)}, u32[]{:S(2)}, u32[]{:S(2)}) collective-permute-start(bf16[256,128]{1,0:T(8,128)(2,1)S(1)} %get-tuple-element.22.rest_0_), channel_id=1, source_target_pairs={{8,0},{0,8},{24,16},{16,24},{9,1},{1,9},{25,17},{17,25},{10,2},{2,... | collective-permute-start | bytes 196616 | tf_op jit(solution)/shard_map/ppermute | solution.py:317
  8.8 5.8 %collective-permute-start.2 = (bf16[256,128]{1,0:T(8,128)(2,1)S(1)}, bf16[256,128]{1,0:T(8,128)(2,1)S(1)}, u32[]{:S(2)}, u32[]{:S(2)}) collective-permute-start(bf16[256,128]{1,0:T(8,128)(2,1)S(1)} %collective-permute-done.1.rest_2_), channel_id=1, source_target_pairs={{8,0},{0,8},{24,16},{16,24},{9,1},{1,9},{25,17},{17,25},{10,2},{2,... | collective-permute-start | bytes 196616 | tf_op jit(solution)/shard_map/ppermute | solution.py:336
  10.2 13.0 %collective-permute-start.5 = (bf16[256,128]{1,0:T(8,128)(2,1)S(1)}, bf16[256,128]{1,0:T(8,128)(2,1)S(1)}, u32[]{:S(2)}, u32[]{:S(2)}) collective-permute-start(bf16[256,128]{1,0:T(8,128)(2,1)S(1)} %get-tuple-element.26.rest_0_), channel_id=1, source_target_pairs={{24,0},{16,8},{8,16},{0,24},{25,1},{17,9},{9,17},{1,25},{26,2},{18... | collective-permute-start | bytes 196616 | tf_op jit(solution)/shard_map/ppermute | solution.py:317
  12.9 10.3 %collective-permute-start.4 = (bf16[256,128]{1,0:T(8,128)(2,1)S(1)}, bf16[256,128]{1,0:T(8,128)(2,1)S(1)}, u32[]{:S(2)}, u32[]{:S(2)}) collective-permute-start(bf16[256,128]{1,0:T(8,128)(2,1)S(1)} %get-tuple-element.26.rest_0_), channel_id=1, source_target_pairs={{16,0},{24,8},{0,16},{8,24},{17,1},{25,9},{1,17},{9,25},{18,2},{26... | collective-permute-start | bytes 196616 | tf_op jit(solution)/shard_map/ppermute | solution.py:317
  13.3 9.8 %collective-permute-start.3 = (bf16[256,128]{1,0:T(8,128)(2,1)S(1)}, bf16[256,128]{1,0:T(8,128)(2,1)S(1)}, u32[]{:S(2)}, u32[]{:S(2)}) collective-permute-start(bf16[256,128]{1,0:T(8,128)(2,1)S(1)} %get-tuple-element.26.rest_0_), channel_id=1, source_target_pairs={{8,0},{0,8},{24,16},{16,24},{9,1},{1,9},{25,17},{17,25},{10,2},{2,... | collective-permute-start | bytes 196616 | tf_op jit(solution)/shard_map/ppermute | solution.py:317
  20.8 10.3 %collective-permute-start.6 = (bf16[512,128]{1,0:T(8,128)(2,1)S(1)}, bf16[512,128]{1,0:T(8,128)(2,1)S(1)}, u32[]{:S(2)}, u32[]{:S(2)}) collective-permute-start(bf16[512,128]{1,0:T(8,128)(2,1)S(1)} %pad_maximum_fusion.1), channel_id=1, source_target_pairs={{16,0},{24,8},{0,16},{8,24},{17,1},{25,9},{1,17},{9,25},{18,2},{26... | collective-permute-start | bytes 393224 | tf_op jit(solution)/shard_map/ppermute | solution.py:317
  28.7 2.3 %copy-start = (bf16[5,256,2048]{2,1,0:T(8,128)(2,1)}, bf16[5,256,2048]{2,1,0:T(8,128)(2,1)S(1)}, u32[]{:S(2)}) copy-start(bf16[5,256,2048]{2,1,0:T(8,128)(2,1)S(1)} %get-tuple-element.28.ds_ref) | copy-start | bytes 15728644
  31.1 8.1 %collective-permute-start.7 = (bf16[512,128]{1,0:T(8,128)(2,1)S(1)}, bf16[512,128]{1,0:T(8,128)(2,1)S(1)}, u32[]{:S(2)}, u32[]{:S(2)}) collective-permute-start(bf16[512,128]{1,0:T(8,128)(2,1)S(1)} %pad_maximum_fusion.2), channel_id=1, source_target_pairs={{8,0},{0,8},{24,16},{16,24},{9,1},{1,9},{25,17},{17,25},{10,2},{2,... | collective-permute-start | bytes 393224 | tf_op jit(solution)/shard_map/ppermute | solution.py:317
  32.7 6.5 %collective-permute-start.8 = (bf16[256,128]{1,0:T(8,128)(2,1)S(1)}, bf16[256,128]{1,0:T(8,128)(2,1)S(1)}, u32[]{:S(2)}, u32[]{:S(2)}) collective-permute-start(bf16[256,128]{1,0:T(8,128)(2,1)S(1)} %get-tuple-element.35), channel_id=1, source_target_pairs={{16,0},{24,8},{0,16},{8,24},{17,1},{25,9},{1,17},{9,25},{18,2},{26... | collective-permute-start | bytes 196616 | tf_op jit(solution)/shard_map/ppermute | solution.py:317
  32.8 6.5 %collective-permute-start.9 = (bf16[256,128]{1,0:T(8,128)(2,1)S(1)}, bf16[256,128]{1,0:T(8,128)(2,1)S(1)}, u32[]{:S(2)}, u32[]{:S(2)}) collective-permute-start(bf16[256,128]{1,0:T(8,128)(2,1)S(1)} %get-tuple-element.36), channel_id=1, source_target_pairs={{24,0},{16,8},{8,16},{0,24},{25,1},{17,9},{9,17},{1,25},{26,2},{18... | collective-permute-start | bytes 196616 | tf_op jit(solution)/shard_map/ppermute | solution.py:317
  40.0 9.2 %all-to-all-start = ((bf16[8,32,256]{2,1,0:T(8,128)(2,1)}), bf16[8,32,256]{2,1,0:T(8,128)(2,1)S(1)}, u32[]{:S(2)}, u32[]{:S(2)}) async-start(bf16[8,32,256]{2,1,0:T(8,128)(2,1)} %bitcast.1), calls=%async_computation | async-start | bytes 262144 | tf_op jit(solution)/shard_map/all_to_all | solution.py:378
  43.7 2.5 %copy-start.1 = (bf16[5,256,2048]{2,1,0:T(8,128)(2,1)S(1)}, bf16[5,256,2048]{2,1,0:T(8,128)(2,1)}, u32[]{:S(2)}) copy-start(bf16[5,256,2048]{2,1,0:T(8,128)(2,1)} %copy-done) | copy-start | bytes 15728644

commit v4 on v3

--- a/solution.py
+++ b/solution.py
@@ -98,33 +98,20 @@
                 rows = pl.ds(pl.multiple_of(pos * self.span, self.span), self.span)
                 out[rows, :] = shard[half * self.span : (half + 1) * self.span, :]
 
-    def unsort(self, total, outs):
+    def unsort(self, acc, outs, scale):
         for r, out in enumerate(outs):
             dest = partner(self.ctx, r, self.n_ctx)
             for half in range(2):
-                pos = self.position(dest, half)
-                rows = pl.ds(pl.multiple_of(pos * self.span, self.span), self.span)
-                out[half * self.span : (half + 1) * self.span, :] = total(rows)
-
-    def queries(self, ref, row, cols):
-        return jnp.concatenate(
-            [
-                ref[pl.ds(row, self.span), c : c + HEAD_DIM]
-                for c in range(cols.start, cols.stop, HEAD_DIM)
-            ],
-            axis=0,
-        )
-
-    def slot_queries(self, ref, cols):
-        pair = {k: self.queries(ref, self.row[k], cols) for k in (True, False)}
-        out = []
-        for t in range(self.slots):
-            if self.kind(t) is None:
-                row = pl.multiple_of(self.pick(t, self.row), self.span)
-                out.append(self.queries(ref, row, cols))
-            else:
-                out.append(pair[self.kind(t)])
-        return pair, out
+                block = acc[self.position(dest, half)] * scale
+                out[half * self.span : (half + 1) * self.span, :] = block.T.astype(BF16)
+
+    def side(self, t):
+        return self.pick(t, {True: 0, False: 1})
+
+    def add(self, acc, t, part):
+        block = 2 * self.key_tile(t)
+        acc[block] += part[:, : self.span]
+        acc[block + 1] += part[:, self.span :]
 
 
 def pipeline(stages, parts):
@@ -164,62 +151,77 @@
     )(own)
 
 
-def forward_kernel(n_ctx, span, heads, meta, q_ref, g_ref, *rest):
+def prepare_kernel(n_ctx, span, heads, meta, q_ref, g_ref, qt_ref, gt_ref):
+    plan = Plan(n_ctx, span, meta)
+    d = HEAD_DIM
+    for src, dst in ((q_ref, qt_ref), (g_ref, gt_ref)):
+        for kind, side in ((True, 0), (False, 1)):
+            for h in range(src.shape[1] // d):
+                block = src[pl.ds(plan.row[kind], span), h * d : (h + 1) * d]
+                dst[side, :, h * span : (h + 1) * span] = block.astype(F32).T.astype(BF16)
+
+
+def forward_kernel(n_ctx, span, heads, meta, qt_ref, gt_ref, *rest):
     shards = rest[:n_ctx]
     p_ref, inv_ref, gs_ref, k_ref = rest[n_ctx : n_ctx + 4]
     dv_refs = rest[n_ctx + 4 : 2 * n_ctx + 4]
-    s_ref, acc_ref = rest[2 * n_ctx + 4 :]
+    acc_ref, limit_ref = rest[2 * n_ctx + 4 :]
     plan = Plan(n_ctx, span, meta)
-    d = HEAD_DIM
     plan.sort(shards, k_ref)
     acc_ref[...] = jnp.zeros_like(acc_ref)
-    width = heads * span
-    diff = lax.broadcasted_iota(jnp.int32, (plan.tile, width), 0) - lax.rem(
-        lax.broadcasted_iota(jnp.int32, (plan.tile, width), 1), span
-    )
+    first_masked = plan.sure_hi - 1
+    dims = (plan.tile, span)
+    diff = lax.broadcasted_iota(jnp.int32, dims, 0) - lax.broadcasted_iota(jnp.int32, dims, 1)
+    for t in range(first_masked, plan.slots):
+        position = plan.pick(t, {True: plan.hi, False: plan.lo})
+        seen = diff <= position * span - plan.key_tile(t) * plan.tile
+        limit_ref[t - first_masked] = jnp.where(seen, jnp.inf, -jnp.inf)
+
+    def rows_of_eight(x):
+        return x.reshape(x.shape[0] // 8, 8, x.shape[1])
 
     def score(cols, state):
         state["tops"] = tops = {True: None, False: None}
-        _, qs = plan.slot_queries(q_ref, cols)
-        for t in range(plan.slots):
-            s = dot_nt(k_ref[plan.keys(t), :], qs[t])
-            if t >= plan.sure_hi - 1:
-                position = plan.pick(t, {True: plan.hi, False: plan.lo})
-                limit = position * span - plan.key_tile(t) * plan.tile
-                s = jnp.where(diff <= limit, s, -jnp.inf)
-            s_ref[t, :, cols] = s
-            plan.fold(tops, t, jnp.max(s, axis=0, keepdims=True), jnp.maximum, -jnp.inf)
+        for t in range(plan.slots):
+            s = dot_nn(k_ref[plan.keys(t), :], qt_ref[plan.side(t), :, cols])
+            if t >= first_masked:
+                s = jnp.minimum(s, jnp.concatenate([limit_ref[t - first_masked]] * heads, axis=1))
+            p_ref[t, :, cols] = s
+            plan.fold(tops, t, jnp.max(rows_of_eight(s), axis=0), jnp.maximum, -jnp.inf)
             yield
+        for kind in (True, False):
+            tops[kind] = jnp.max(tops[kind], axis=0, keepdims=True)
 
     def exponent(cols, state):
         tops = state["tops"]
         sums = {True: None, False: None}
         for t in range(plan.slots):
-            p = jnp.exp2((s_ref[t, :, cols] - plan.pick(t, tops)) * EXP_SCALE)
-            p_ref[t, :, cols] = p.astype(BF16)
-            plan.fold(sums, t, jnp.sum(p, axis=0, keepdims=True), jnp.add, 0.0)
+            top = plan.pick(t, tops)
+            parts = []
+            for h in range(heads):
+                here = slice(cols.start + h * span, cols.start + (h + 1) * span)
+                s = p_ref[t, :, here] - top[:, h * span : (h + 1) * span]
+                p = jnp.exp2(s * EXP_SCALE)
+                p_ref[t, :, here] = p
+                parts.append(jnp.sum(rows_of_eight(p), axis=0))
+            plan.fold(sums, t, jnp.concatenate(parts, axis=1), jnp.add, 0.0)
             yield
-        for kind, r in ((True, 0), (False, 1)):
-            inverse = 1.0 / sums[kind]
-            inv_ref[r : r + 1, cols] = inverse
-            for h in range(heads):
-                here = slice(cols.start + h * d, cols.start + (h + 1) * d)
-                row = inverse[:, h * span : (h + 1) * span]
-                column = jnp.broadcast_to(row, (span, span)).T
-                g = g_ref[pl.ds(plan.row[kind], span), here].astype(F32)
-                gs_ref[pl.ds(plan.row[kind], span), here] = (g * column).astype(BF16)
+        for kind, side in ((True, 0), (False, 1)):
+            inverse = 1.0 / jnp.sum(sums[kind], axis=0, keepdims=True)
+            inv_ref[side : side + 1, cols] = inverse
+            gs_ref[side, :, cols] = (gt_ref[side, :, cols].astype(F32) * inverse).astype(BF16)
 
     def value(cols, state):
-        _, gs = plan.slot_queries(gs_ref, cols)
-        for t in range(plan.slots):
-            acc_ref[plan.keys(t), :] += dot_nn(p_ref[t, :, cols], gs[t])
+        for t in range(plan.slots):
+            p = p_ref[t, :, cols].astype(BF16)
+            plan.add(acc_ref, t, dot_nt(gs_ref[plan.side(t), :, cols], p))
             yield
 
-    pipeline((score, exponent, value), groups(q_ref.shape[1], heads))
-    plan.unsort(lambda rows: acc_ref[rows, :].astype(BF16), dv_refs)
-
-
-def backward_kernel(n_ctx, span, heads, meta, p_ref, inv_ref, gs_ref, q_ref, *rest):
+    pipeline((score, exponent, value), groups(qt_ref.shape[2], heads))
+    plan.unsort(acc_ref, dv_refs, 1.0)
+
+
+def backward_kernel(n_ctx, span, heads, meta, p_ref, inv_ref, gs_ref, qt_ref, *rest):
     shards = rest[:n_ctx]
     o_ref, ds_ref = rest[n_ctx : n_ctx + 2]
     dk_refs = rest[n_ctx + 2 : 2 * n_ctx + 2]
@@ -234,34 +236,30 @@
     def output(cols, state):
         outs = {True: None, False: None}
         for t in range(plan.slots):
-            part = dot_nn(vt_ref[plan.key_tile(t)], p_ref[t, :, cols])
+            part = dot_nn(vt_ref[plan.key_tile(t)], p_ref[t, :, cols].astype(BF16))
             plan.fold(outs, t, part, jnp.add, 0.0)
             yield
         state["dots"] = dots = {}
-        for kind, r in ((True, 0), (False, 1)):
-            out = outs[kind] * inv_ref[r : r + 1, cols]
-            parts = []
+        for kind, side in ((True, 0), (False, 1)):
+            out = outs[kind] * inv_ref[side : side + 1, cols]
             for h in range(heads):
                 here = slice(cols.start + h * d, cols.start + (h + 1) * d)
                 o = out[:, h * span : (h + 1) * span].T.astype(BF16)
                 o_ref[pl.ds(plan.row[kind], span), here] = o
-                g = gs_ref[pl.ds(plan.row[kind], span), here].astype(F32)
-                parts.append(jnp.sum((g * o.astype(F32)).T, axis=0, keepdims=True))
-            dots[kind] = jnp.concatenate(parts, axis=1)
+            prod = gs_ref[side, :, cols].astype(F32) * out.astype(BF16).astype(F32)
+            dots[kind] = jnp.sum(prod, axis=0, keepdims=True)
 
     def score_grad(cols, state):
-        _, qs = plan.slot_queries(q_ref, cols)
-        _, gs = plan.slot_queries(gs_ref, cols)
-        for t in range(plan.slots):
-            dp = dot_nt(v_ref[plan.keys(t), :], gs[t])
+        for t in range(plan.slots):
+            dp = dot_nn(v_ref[plan.keys(t), :], gs_ref[plan.side(t), :, cols])
             dots = plan.pick(t, state["dots"])
-            ds = (p_ref[t, :, cols].astype(F32) * (dp - dots)).astype(BF16)
+            ds = (p_ref[t, :, cols] * (dp - dots)).astype(BF16)
             ds_ref[t, :, cols] = ds
-            acc_ref[plan.keys(t), :] += dot_nn(ds, qs[t])
+            plan.add(acc_ref, t, dot_nt(qt_ref[plan.side(t), :, cols], ds))
             yield
 
-    pipeline((output, score_grad), groups(q_ref.shape[1], heads))
-    plan.unsort(lambda rows: (acc_ref[rows, :] * SCALE).astype(BF16), dk_refs)
+    pipeline((output, score_grad), groups(qt_ref.shape[2], heads))
+    plan.unsort(acc_ref, dk_refs, SCALE)
 
 
 def query_kernel(n_ctx, span, heads, meta, ds_ref, k_ref, dq_ref, kt_ref):
@@ -341,19 +339,22 @@
     rows, pair, shard = shape((tokens, width)), shape((2, q_heads * span), F32), shape((tokens, d))
     work = 2 * slots[0] * slots[1] * slots[2] * d
     bind = lambda f: functools.partial(f, n_ctx, span, heads)
+    turned = shape((2, d, q_heads * span))
+    total_shape = pltpu.VMEM((2 * n_ctx, d, span), F32)
+    queries, grads = call(
+        bind(prepare_kernel), [turned, turned], [], work // 10,
+    )(order, query_rows, out_grad)
     p, inverse, grads, key_sorted, *value_parts = call(
         bind(forward_kernel),
-        [shape(slots), pair, rows, shape((keys, d))] + [shard] * n_ctx,
-        [pltpu.VMEM(slots, F32), pltpu.VMEM((keys, d), F32)], 2 * work,
-    )(order, query_rows, out_grad, *key_shards)
+        [shape(slots, F32), pair, turned, shape((keys, d))] + [shard] * n_ctx,
+        [total_shape, pltpu.VMEM((n_ctx + 2 - (n_ctx + 2) // 2, tokens, span), F32)],
+        2 * work,
+    )(order, queries, grads, *key_shards)
     attn_out, score_grads, *key_parts = call(
         bind(backward_kernel), [rows, shape(slots)] + [shard] * n_ctx,
-        [
-            pltpu.VMEM((keys, d), BF16),
-            pltpu.VMEM((n_ctx, d, tokens), BF16),
-            pltpu.VMEM((keys, d), F32),
-        ], 3 * work,
-    )(order, p, inverse, grads, query_rows, *value_shards)
+        [pltpu.VMEM((keys, d), BF16), pltpu.VMEM((n_ctx, d, tokens), BF16), total_shape],
+        3 * work,
+    )(order, p, inverse, grads, queries, *value_shards)
     (query_grad,) = call(
         bind(query_kernel), [rows],
         [pltpu.VMEM((n_ctx, d, tokens), BF16)], work,

time: 50.2 us -> 49.7 us (0.990)
    pallas_call x3 -> x4, Pallas kernels: 13.9 us -> 13.8 us  [run(): pl.pallas_call(body, in_specs=[vmem] * (1 + len(args)), out_specs=[vmem]...]
where the time goes in v4:
time: 49.7 us; the launch traced here: 49.4 us
  starting transfers between devices  22 us (44%)
  Pallas kernels  14.5 us (29%)
  local copies, waits for them, and re-layouts  5.71 us (11%)
  waiting for transfers between devices  5.65 us (11%)
  other arithmetic  0.79 us (2%)
  between operations  0.77 us (2%)
    ppermute x9, starting transfers between devices, shift(): return lax.ppermute(a, 'ctx', [p[::-1] for p in pairs] if back else pairs)  16.9 us
    pallas_call x4, Pallas kernels, run(): pl.pallas_call(body, in_specs=[vmem] * (1 + len(args)), out_specs=[vmem]...  13.8 us
    unnamed x10, local copies, waits for them, and re-layouts  4.83 us
    ppermute x9, waiting for transfers between devices, shift(): return lax.ppermute(a, 'ctx', [p[::-1] for p in pairs] if back else pairs)  4.81 us
    all_to_all x1, starting transfers between devices, per_device(): lax.all_to_all(owned.reshape(n_head, rows_out, 2 * d), 'head', split_axis...  3.72 us
    ppermute x1, starting transfers between devices, gather(): across = lax.ppermute(far, 'ctx', [(i ^ 1, i) for i in range(n_ctx)])  1.37 us
  transfers between devices with their start and end apart: 11, of which 3 were waited for; matrix products, arithmetic and copies ran while one was open for 0% of the time, Pallas kernels for 28%

profile of v4, /device:TPU:0, one launch (start us, length us, event | category | flops | bytes accessed | tf_op | source)
XLA Modules:
  0.0 49.4 jit_solution(6838394882771817640)
XLA Ops:
  0.6 0.9 %constant_dynamic-slice_fusion = (bf16[256,128]{1,0:T(8,128)(2,1)S(1)}, bf16[256,128]{1,0:T(8,128)(2,1)S(1)}) fusion(bf16[256,1024]{1,0:T(8,128)(2,1)} %param.7, s32[]{:T(128)S(6)} %select_n.10, bf16[256,1024]{1,0:T(8,128)(2,1)} %param.6), kind=kLoop, calls=%fused_computation.7 | loop fusion | bytes 262148 | tf_op jit(solution)/shard_map/dynamic_slice | solution.py:325
  1.6 0.0 copy-start.2
  1.6 0.0 copy-start.3
  1.6 0.0 copy-start.4
  1.6 4.1 %collective-permute-start.1 = (bf16[256,128]{1,0:T(8,128)(2,1)S(1)}, bf16[256,128]{1,0:T(8,128)(2,1)S(1)}, u32[]{:S(2)}, u32[]{:S(2)}) collective-permute-start(bf16[256,128]{1,0:T(8,128)(2,1)S(1)} %get-tuple-element.26.rest_0_), channel_id=1, source_target_pairs={{16,0},{24,8},{0,16},{8,24},{17,1},{25,9},{1,17},{9,25},{18,2},{26... | collective-permute-start | bytes 196616 | tf_op jit(solution)/shard_map/ppermute | solution.py:315
  5.7 1.6 %collective-permute-start = (bf16[256,128]{1,0:T(8,128)(2,1)S(1)}, bf16[256,128]{1,0:T(8,128)(2,1)S(1)}, u32[]{:S(2)}, u32[]{:S(2)}) collective-permute-start(bf16[256,128]{1,0:T(8,128)(2,1)S(1)} %get-tuple-element.26.rest_0_), channel_id=1, source_target_pairs={{8,0},{0,8},{24,16},{16,24},{9,1},{1,9},{25,17},{17,25},{10,2},{2,... | collective-permute-start | bytes 196616 | tf_op jit(solution)/shard_map/ppermute | solution.py:315
  7.3 1.5 %collective-permute-done.1.rest_2_ = bf16[256,128]{1,0:T(8,128)(2,1)S(1)} collective-permute-done((bf16[256,128]{1,0:T(8,128)(2,1)S(1)}, bf16[256,128]{1,0:T(8,128)(2,1)S(1)}, u32[]{:S(2)}, u32[]{:S(2)}) %collective-permute-start.1) | collective-permute-done | bytes 65568 | tf_op jit(solution)/shard_map/ppermute | solution.py:315
  8.8 1.4 %collective-permute-start.2 = (bf16[256,128]{1,0:T(8,128)(2,1)S(1)}, bf16[256,128]{1,0:T(8,128)(2,1)S(1)}, u32[]{:S(2)}, u32[]{:S(2)}) collective-permute-start(bf16[256,128]{1,0:T(8,128)(2,1)S(1)} %collective-permute-done.1.rest_2_), channel_id=1, source_target_pairs={{8,0},{0,8},{24,16},{16,24},{9,1},{1,9},{25,17},{17,25},{10,2},{2,... | collective-permute-start | bytes 196616 | tf_op jit(solution)/shard_map/ppermute | solution.py:334
  10.2 2.7 %collective-permute-start.5 = (bf16[256,128]{1,0:T(8,128)(2,1)S(1)}, bf16[256,128]{1,0:T(8,128)(2,1)S(1)}, u32[]{:S(2)}, u32[]{:S(2)}) collective-permute-start(bf16[256,128]{1,0:T(8,128)(2,1)S(1)} %get-tuple-element.30.rest_0_), channel_id=1, source_target_pairs={{24,0},{16,8},{8,16},{0,24},{25,1},{17,9},{9,17},{1,25},{26,2},{18... | collective-permute-start | bytes 196616 | tf_op jit(solution)/shard_map/ppermute | solution.py:315
  12.9 0.4 collective-permute-start.4
  13.3 1.2 %collective-permute-start.3 = (bf16[256,128]{1,0:T(8,128)(2,1)S(1)}, bf16[256,128]{1,0:T(8,128)(2,1)S(1)}, u32[]{:S(2)}, u32[]{:S(2)}) collective-permute-start(bf16[256,128]{1,0:T(8,128)(2,1)S(1)} %get-tuple-element.30.rest_0_), channel_id=1, source_target_pairs={{8,0},{0,8},{24,16},{16,24},{9,1},{1,9},{25,17},{17,25},{10,2},{2,... | collective-permute-start | bytes 196616 | tf_op jit(solution)/shard_map/ppermute | solution.py:315
  14.6 0.0 copy-done.2
  14.6 0.0 copy-done.3
  14.6 0.0 copy-done.4
  14.6 0.7 %shard_map.84 = (bf16[2,128,2048]{2,1,0:T(8,128)(2,1)S(1)}, bf16[2,128,2048]{2,1,0:T(8,128)(2,1)S(1)}) custom-call(s32[1,8]{1,0:T(1,128)S(1)} %bitcast.4, bf16[256,2048]{1,0:T(8,128)(2,1)S(1)} %copy-done.2, bf16[256,2048]{1,0:T(8,128)(2,1)S(1)} %copy-done.3), custom_call_target="tpu_custom_call" | custom-call | flops 67108864 | bytes 131072 | tf_op jit(solution)/shard_map/pallas_call | solution.py:286
  15.3 0.0 collective-permute-done.rest_1_
  15.3 0.0 collective-permute-done.2.rest_3_
  15.3 5.6 %shard_map.85 = (f32[5,256,2048]{2,1,0:T(8,128)S(1)}, f32[2,2048]{1,0:T(2,128)S(1)}, bf16[2,128,2048]{2,1,0:T(8,128)(2,1)S(1)}, bf16[1024,128]{1,0:T(8,128)(2,1)...) custom-call(s32[1,8]{1,0:T(1,128)S(1)} %bitcast.5, ...), custom_call_target="tpu_custom_call" | custom-call | flops 1342177280 | bytes 2621440 | tf_op jit(solution)/shard_map/pallas_call | solution.py:286
  21.0 2.3 %collective-permute-start.6 = (bf16[512,128]{1,0:T(8,128)(2,1)S(1)}, bf16[512,128]{1,0:T(8,128)(2,1)S(1)}, u32[]{:S(2)}, u32[]{:S(2)}) collective-permute-start(bf16[512,128]{1,0:T(8,128)(2,1)S(1)} %pad_maximum_fusion.1), channel_id=1, source_target_pairs={{16,0},{24,8},{0,16},{8,24},{17,1},{25,9},{1,17},{9,25},{18,2},{26... | collective-permute-start | bytes 393224 | tf_op jit(solution)/shard_map/ppermute | solution.py:315
  23.3 0.0 collective-permute-done.5.rest_3_
  23.3 0.0 collective-permute-done.4.rest_2_
  23.3 0.0 collective-permute-done.3.rest_1_
  23.3 5.3 %shard_map.86 = (bf16[256,2048]{1,0:T(8,128)(2,1)}, bf16[5,256,2048]{2,1,0:T(8,128)(2,1)S(1)}, bf16[256,128]{1,0:T(8,128)(2,1)S(1)}, bf16[256,128]{1,0:T(8,128)(...) custom-call(s32[1,8]{1,0:T(1,128)S(1)} %bitcast.6, f32[5,256,2048]{2,1,0:T(8,128)S(1)} %get-tuple-element.27.p_ref, ...), custom_call_target="tpu_custom_call" | custom-call | flops 2013265920 | bytes 3932160 | tf_op jit(solution)/shard_map/pallas_call | solution.py:286
  28.6 0.0 copy-start
  28.6 2.3 %copy-done = bf16[5,256,2048]{2,1,0:T(8,128)(2,1)} copy-done((bf16[5,256,2048]{2,1,0:T(8,128)(2,1)}, bf16[5,256,2048]{2,1,0:T(8,128)(2,1)S(1)}, u32[]{:S(2)}) %copy-start) | copy-done | bytes 5242904
  30.9 0.0 collective-permute-done.6
  31.0 1.1 %collective-permute-start.7 = (bf16[512,128]{1,0:T(8,128)(2,1)S(1)}, bf16[512,128]{1,0:T(8,128)(2,1)S(1)}, u32[]{:S(2)}, u32[]{:S(2)}) collective-permute-start(bf16[512,128]{1,0:T(8,128)(2,1)S(1)} %pad_maximum_fusion.2), channel_id=1, source_target_pairs={{8,0},{0,8},{24,16},{16,24},{9,1},{1,9},{25,17},{17,25},{10,2},{2,... | collective-permute-start | bytes 393224 | tf_op jit(solution)/shard_map/ppermute | solution.py:315
  32.1 0.4 collective-permute-start.8
  32.5 2.9 %collective-permute-start.9 = (bf16[256,128]{1,0:T(8,128)(2,1)S(1)}, bf16[256,128]{1,0:T(8,128)(2,1)S(1)}, u32[]{:S(2)}, u32[]{:S(2)}) collective-permute-start(bf16[256,128]{1,0:T(8,128)(2,1)S(1)} %get-tuple-element.40), channel_id=1, source_target_pairs={{24,0},{16,8},{8,16},{0,24},{25,1},{17,9},{9,17},{1,25},{26,2},{18... | collective-permute-start | bytes 196616 | tf_op jit(solution)/shard_map/ppermute | solution.py:315
  35.4 3.3 %collective-permute-done.8 = bf16[256,128]{1,0:T(8,128)(2,1)S(1)} collective-permute-done((bf16[256,128]{1,0:T(8,128)(2,1)S(1)}, bf16[256,128]{1,0:T(8,128)(2,1)S(1)}, u32[]{:S(2)}, u32[]{:S(2)}) %collective-permute-start.8) | collective-permute-done | bytes 65568 | tf_op jit(solution)/shard_map/ppermute | solution.py:315
  38.8 0.0 collective-permute-done.9
  38.8 0.0 collective-permute-done.7
  38.8 0.1 add_convert_fusion.1
  38.8 0.7 %pad_maximum_fusion.3 = bf16[256,256]{1,0:T(8,128)(2,1)} fusion(bf16[256,128]{1,0:T(8,128)(2,1)S(1)} %get-tuple-element.45, bf16[256,128]{1,0:T(8,128)(2,1)S(1)} %get-tuple-element.44), kind=kLoop, calls=%fused_computation.3 | loop fusion | flops 262144 | bytes 262144 | tf_op jit(solution)/shard_map/concatenate | solution.py:378
  39.5 3.7 %all-to-all-start = ((bf16[8,32,256]{2,1,0:T(8,128)(2,1)}), bf16[8,32,256]{2,1,0:T(8,128)(2,1)S(1)}, u32[]{:S(2)}, u32[]{:S(2)}) async-start(bf16[8,32,256]{2,1,0:T(8,128)(2,1)} %bitcast.1), calls=%async_computation | async-start | bytes 262144 | tf_op jit(solution)/shard_map/all_to_all | solution.py:379
  43.2 0.0 copy-start.1
  43.2 2.5 %copy-done.1 = bf16[5,256,2048]{2,1,0:T(8,128)(2,1)S(1)} copy-done((bf16[5,256,2048]{2,1,0:T(8,128)(2,1)S(1)}, bf16[5,256,2048]{2,1,0:T(8,128)(2,1)}, u32[]{:S(2)}) %copy-start.1) | copy-done | bytes 5242904
  45.7 2.2 %shard_map.87 = bf16[256,2048]{1,0:T(8,128)(2,1)} custom-call(s32[1,8]{1,0:T(1,128)S(1)} %bitcast.7, bf16[5,256,2048]{2,1,0:T(8,128)(2,1)S(1)} %copy-done.1, bf16[1024,128]{1,0:T(8,128)(2,1)S(1)} %get-tuple-element.33.k_ref), custom_call_target="tpu_custom_call" | custom-call | flops 671088640 | bytes 1310720 | tf_op jit(solution)/shard_map/pallas_call | solution.py:286
  47.9 0.8 %all-to-all-done = bf16[8,32,256]{2,1,0:T(8,128)(2,1)S(1)} async-done(((bf16[8,32,256]{2,1,0:T(8,128)(2,1)}), bf16[8,32,256]{2,1,0:T(8,128)(2,1)S(1)}, u32[]{:S(2)}, u32[]{:S(2)}) %all-to-all-start) | async-done | bytes 131104 | tf_op jit(solution)/shard_map/all_to_all | solution.py:379
  48.7 0.7 %total.1 = (bf16[32,1024]{1,0:T(8,128)(2,1)}, bf16[32,1024]{1,0:T(8,128)(2,1)}) custom-call(bf16[8,1,32,256]{3,2,1,0:T(8,128)(2,1)S(1)} %bitcast.3), custom_call_target="tpu_custom_call" | custom-call | tf_op jit(solution)/shard_map/total/pallas_call | solution.py:398
  (5 shorter events, 0.1 us)
Async XLA Ops:
  1.6 13.0 %copy-start.2 = (bf16[256,2048]{1,0:T(8,128)(2,1)S(1)}, bf16[256,2048]{1,0:T(8,128)(2,1)}, u32[]{:S(2)}) copy-start(bf16[256,2048]{1,0:T(8,128)(2,1)} %q_ref.1) | copy-start | bytes 3145732
  1.6 13.0 %copy-start.3 = (bf16[256,2048]{1,0:T(8,128)(2,1)S(1)}, bf16[256,2048]{1,0:T(8,128)(2,1)}, u32[]{:S(2)}) copy-start(bf16[256,2048]{1,0:T(8,128)(2,1)} %g_ref.1) | copy-start | bytes 3145732
  1.6 13.0 %copy-start.4 = (s32[8]{0:T(128)S(1)}, s32[8]{0:T(128)}, u32[]{:S(2)}) copy-start(s32[8]{0:T(128)} %param.9) | copy-start | bytes 100
  1.6 7.2 %collective-permute-start.1 = (bf16[256,128]{1,0:T(8,128)(2,1)S(1)}, bf16[256,128]{1,0:T(8,128)(2,1)S(1)}, u32[]{:S(2)}, u32[]{:S(2)}) collective-permute-start(bf16[256,128]{1,0:T(8,128)(2,1)S(1)} %get-tuple-element.26.rest_0_), channel_id=1, source_target_pairs={{16,0},{24,8},{0,16},{8,24},{17,1},{25,9},{1,17},{9,25},{18,2},{26... | collective-permute-start | bytes 196616 | tf_op jit(solution)/shard_map/ppermute | solution.py:315
  5.7 9.6 %collective-permute-start = (bf16[256,128]{1,0:T(8,128)(2,1)S(1)}, bf16[256,128]{1,0:T(8,128)(2,1)S(1)}, u32[]{:S(2)}, u32[]{:S(2)}) collective-permute-start(bf16[256,128]{1,0:T(8,128)(2,1)S(1)} %get-tuple-element.26.rest_0_), channel_id=1, source_target_pairs={{8,0},{0,8},{24,16},{16,24},{9,1},{1,9},{25,17},{17,25},{10,2},{2,... | collective-permute-start | bytes 196616 | tf_op jit(solution)/shard_map/ppermute | solution.py:315
  8.8 6.5 %collective-permute-start.2 = (bf16[256,128]{1,0:T(8,128)(2,1)S(1)}, bf16[256,128]{1,0:T(8,128)(2,1)S(1)}, u32[]{:S(2)}, u32[]{:S(2)}) collective-permute-start(bf16[256,128]{1,0:T(8,128)(2,1)S(1)} %collective-permute-done.1.rest_2_), channel_id=1, source_target_pairs={{8,0},{0,8},{24,16},{16,24},{9,1},{1,9},{25,17},{17,25},{10,2},{2,... | collective-permute-start | bytes 196616 | tf_op jit(solution)/shard_map/ppermute | solution.py:334
  10.2 13.2 %collective-permute-start.5 = (bf16[256,128]{1,0:T(8,128)(2,1)S(1)}, bf16[256,128]{1,0:T(8,128)(2,1)S(1)}, u32[]{:S(2)}, u32[]{:S(2)}) collective-permute-start(bf16[256,128]{1,0:T(8,128)(2,1)S(1)} %get-tuple-element.30.rest_0_), channel_id=1, source_target_pairs={{24,0},{16,8},{8,16},{0,24},{25,1},{17,9},{9,17},{1,25},{26,2},{18... | collective-permute-start | bytes 196616 | tf_op jit(solution)/shard_map/ppermute | solution.py:315
  12.9 10.4 %collective-permute-start.4 = (bf16[256,128]{1,0:T(8,128)(2,1)S(1)}, bf16[256,128]{1,0:T(8,128)(2,1)S(1)}, u32[]{:S(2)}, u32[]{:S(2)}) collective-permute-start(bf16[256,128]{1,0:T(8,128)(2,1)S(1)} %get-tuple-element.30.rest_0_), channel_id=1, source_target_pairs={{16,0},{24,8},{0,16},{8,24},{17,1},{25,9},{1,17},{9,25},{18,2},{26... | collective-permute-start | bytes 196616 | tf_op jit(solution)/shard_map/ppermute | solution.py:315
  13.3 10.0 %collective-permute-start.3 = (bf16[256,128]{1,0:T(8,128)(2,1)S(1)}, bf16[256,128]{1,0:T(8,128)(2,1)S(1)}, u32[]{:S(2)}, u32[]{:S(2)}) collective-permute-start(bf16[256,128]{1,0:T(8,128)(2,1)S(1)} %get-tuple-element.30.rest_0_), channel_id=1, source_target_pairs={{8,0},{0,8},{24,16},{16,24},{9,1},{1,9},{25,17},{17,25},{10,2},{2,... | collective-permute-start | bytes 196616 | tf_op jit(solution)/shard_map/ppermute | solution.py:315
  21.0 10.0 %collective-permute-start.6 = (bf16[512,128]{1,0:T(8,128)(2,1)S(1)}, bf16[512,128]{1,0:T(8,128)(2,1)S(1)}, u32[]{:S(2)}, u32[]{:S(2)}) collective-permute-start(bf16[512,128]{1,0:T(8,128)(2,1)S(1)} %pad_maximum_fusion.1), channel_id=1, source_target_pairs={{16,0},{24,8},{0,16},{8,24},{17,1},{25,9},{1,17},{9,25},{18,2},{26... | collective-permute-start | bytes 393224 | tf_op jit(solution)/shard_map/ppermute | solution.py:315
  28.6 2.3 %copy-start = (bf16[5,256,2048]{2,1,0:T(8,128)(2,1)}, bf16[5,256,2048]{2,1,0:T(8,128)(2,1)S(1)}, u32[]{:S(2)}) copy-start(bf16[5,256,2048]{2,1,0:T(8,128)(2,1)S(1)} %get-tuple-element.32.ds_ref) | copy-start | bytes 15728644
  31.0 7.8 %collective-permute-start.7 = (bf16[512,128]{1,0:T(8,128)(2,1)S(1)}, bf16[512,128]{1,0:T(8,128)(2,1)S(1)}, u32[]{:S(2)}, u32[]{:S(2)}) collective-permute-start(bf16[512,128]{1,0:T(8,128)(2,1)S(1)} %pad_maximum_fusion.2), channel_id=1, source_target_pairs={{8,0},{0,8},{24,16},{16,24},{9,1},{1,9},{25,17},{17,25},{10,2},{2,... | collective-permute-start | bytes 393224 | tf_op jit(solution)/shard_map/ppermute | solution.py:315
  32.1 6.7 %collective-permute-start.8 = (bf16[256,128]{1,0:T(8,128)(2,1)S(1)}, bf16[256,128]{1,0:T(8,128)(2,1)S(1)}, u32[]{:S(2)}, u32[]{:S(2)}) collective-permute-start(bf16[256,128]{1,0:T(8,128)(2,1)S(1)} %get-tuple-element.39), channel_id=1, source_target_pairs={{16,0},{24,8},{0,16},{8,24},{17,1},{25,9},{1,17},{9,25},{18,2},{26... | collective-permute-start | bytes 196616 | tf_op jit(solution)/shard_map/ppermute | solution.py:315
  32.5 6.2 %collective-permute-start.9 = (bf16[256,128]{1,0:T(8,128)(2,1)S(1)}, bf16[256,128]{1,0:T(8,128)(2,1)S(1)}, u32[]{:S(2)}, u32[]{:S(2)}) collective-permute-start(bf16[256,128]{1,0:T(8,128)(2,1)S(1)} %get-tuple-element.40), channel_id=1, source_target_pairs={{24,0},{16,8},{8,16},{0,24},{25,1},{17,9},{9,17},{1,25},{26,2},{18... | collective-permute-start | bytes 196616 | tf_op jit(solution)/shard_map/ppermute | solution.py:315
  39.5 9.2 %all-to-all-start = ((bf16[8,32,256]{2,1,0:T(8,128)(2,1)}), bf16[8,32,256]{2,1,0:T(8,128)(2,1)S(1)}, u32[]{:S(2)}, u32[]{:S(2)}) async-start(bf16[8,32,256]{2,1,0:T(8,128)(2,1)} %bitcast.1), calls=%async_computation | async-start | bytes 262144 | tf_op jit(solution)/shard_map/all_to_all | solution.py:379
  43.2 2.5 %copy-start.1 = (bf16[5,256,2048]{2,1,0:T(8,128)(2,1)S(1)}, bf16[5,256,2048]{2,1,0:T(8,128)(2,1)}, u32[]{:S(2)}) copy-start(bf16[5,256,2048]{2,1,0:T(8,128)(2,1)} %copy-done) | copy-start | bytes 15728644

commit v5 on v4

--- a/solution.py
+++ b/solution.py
@@ -364,11 +364,11 @@
         return functools.reduce(jnp.add, [a.astype(F32) for a in parts])
 
     if n_ctx == 4:
-        far = shift(jnp.concatenate(value_parts[2:]), 2)
-        near = plus(value_parts[1], far[tokens:]).astype(BF16)
-        near = shift(jnp.concatenate([near, key_parts[1]]), 1)
-        value_sum = plus(value_parts[0], far[:tokens], near[:tokens])
-        key_sum = plus(key_parts[0], near[tokens:], *[shift(key_parts[r], r) for r in (2, 3)])
+        near = shift(jnp.concatenate([value_parts[1], value_parts[3]]), 1)
+        far = plus(value_parts[2], near[tokens:]).astype(BF16)
+        far = shift(jnp.concatenate([far, key_parts[2]]), 2)
+        value_sum = plus(value_parts[0], near[:tokens], far[:tokens])
+        key_sum = plus(key_parts[0], far[tokens:], *[shift(key_parts[r], r) for r in (1, 3)])
     else:
         value_sum, key_sum = [
             plus(parts[0], *[shift(parts[r], r, True) for r in others])

time: 49.7 us -> 50.3 us (1.012)
  waiting for transfers between devices: 5.65 us -> 7.75 us
  starting transfers between devices: 22 us -> 20.5 us
    ppermute x9, waiting for transfers between devices: 4.81 us -> 6.91 us  [shift(): return lax.ppermute(a, 'ctx', [p[::-1] for p in pairs] if back else pairs)]
    ppermute x9, starting transfers between devices: 16.9 us -> 15.4 us  [shift(): return lax.ppermute(a, 'ctx', [p[::-1] for p in pairs] if back else pairs)]
  transfers between devices with their start and end apart: 11 -> 11, of which waited for: 3 -> 5; matrix products, arithmetic and copies ran while one was open for 0% -> 0% of each run, Pallas kernels for 28% -> 28%
where the time goes in v5:
time: 50.3 us; the launch traced here: 50 us
  starting transfers between devices  20.5 us (41%)
  Pallas kernels  14.5 us (29%)
  waiting for transfers between devices  7.75 us (15%)
  local copies, waits for them, and re-layouts  5.71 us (11%)
  other arithmetic  0.79 us (2%)
  between operations  0.76 us (2%)
    ppermute x9, starting transfers between devices, shift(): return lax.ppermute(a, 'ctx', [p[::-1] for p in pairs] if back else pairs)  15.4 us
    pallas_call x4, Pallas kernels, run(): pl.pallas_call(body, in_specs=[vmem] * (1 + len(args)), out_specs=[vmem]...  13.8 us
    ppermute x9, waiting for transfers between devices, shift(): return lax.ppermute(a, 'ctx', [p[::-1] for p in pairs] if back else pairs)  6.91 us
    unnamed x10, local copies, waits for them, and re-layouts  4.83 us
    all_to_all x1, starting transfers between devices, per_device(): lax.all_to_all(owned.reshape(n_head, rows_out, 2 * d), 'head', split_axis...  3.72 us
    ppermute x1, starting transfers between devices, gather(): across = lax.ppermute(far, 'ctx', [(i ^ 1, i) for i in range(n_ctx)])  1.37 us
  transfers between devices with their start and end apart: 11, of which 5 were waited for; matrix products, arithmetic and copies ran while one was open for 0% of the time, Pallas kernels for 28%

profile of v5, /device:TPU:0, one launch (start us, length us, event | category | flops | bytes accessed | tf_op | source)
XLA Modules:
  0.0 50.0 jit_solution(11951056688283125036)
XLA Ops:
  0.6 0.9 %constant_dynamic-slice_fusion = (bf16[256,128]{1,0:T(8,128)(2,1)S(1)}, bf16[256,128]{1,0:T(8,128)(2,1)S(1)}) fusion(bf16[256,1024]{1,0:T(8,128)(2,1)} %param.7, s32[]{:T(128)S(6)} %select_n.10, bf16[256,1024]{1,0:T(8,128)(2,1)} %param.6), kind=kLoop, calls=%fused_computation.7 | loop fusion | bytes 262148 | tf_op jit(solution)/shard_map/dynamic_slice | solution.py:325
  1.6 0.0 copy-start.2
  1.6 0.0 copy-start.3
  1.6 0.0 copy-start.4
  1.6 4.1 %collective-permute-start.1 = (bf16[256,128]{1,0:T(8,128)(2,1)S(1)}, bf16[256,128]{1,0:T(8,128)(2,1)S(1)}, u32[]{:S(2)}, u32[]{:S(2)}) collective-permute-start(bf16[256,128]{1,0:T(8,128)(2,1)S(1)} %get-tuple-element.26.rest_0_), channel_id=1, source_target_pairs={{16,0},{24,8},{0,16},{8,24},{17,1},{25,9},{1,17},{9,25},{18,2},{26... | collective-permute-start | bytes 196616 | tf_op jit(solution)/shard_map/ppermute | solution.py:315
  5.7 1.6 %collective-permute-start = (bf16[256,128]{1,0:T(8,128)(2,1)S(1)}, bf16[256,128]{1,0:T(8,128)(2,1)S(1)}, u32[]{:S(2)}, u32[]{:S(2)}) collective-permute-start(bf16[256,128]{1,0:T(8,128)(2,1)S(1)} %get-tuple-element.26.rest_0_), channel_id=1, source_target_pairs={{8,0},{0,8},{24,16},{16,24},{9,1},{1,9},{25,17},{17,25},{10,2},{2,... | collective-permute-start | bytes 196616 | tf_op jit(solution)/shard_map/ppermute | solution.py:315
  7.3 1.5 %collective-permute-done.1.rest_2_ = bf16[256,128]{1,0:T(8,128)(2,1)S(1)} collective-permute-done((bf16[256,128]{1,0:T(8,128)(2,1)S(1)}, bf16[256,128]{1,0:T(8,128)(2,1)S(1)}, u32[]{:S(2)}, u32[]{:S(2)}) %collective-permute-start.1) | collective-permute-done | bytes 65568 | tf_op jit(solution)/shard_map/ppermute | solution.py:315
  8.8 1.4 %collective-permute-start.2 = (bf16[256,128]{1,0:T(8,128)(2,1)S(1)}, bf16[256,128]{1,0:T(8,128)(2,1)S(1)}, u32[]{:S(2)}, u32[]{:S(2)}) collective-permute-start(bf16[256,128]{1,0:T(8,128)(2,1)S(1)} %collective-permute-done.1.rest_2_), channel_id=1, source_target_pairs={{8,0},{0,8},{24,16},{16,24},{9,1},{1,9},{25,17},{17,25},{10,2},{2,... | collective-permute-start | bytes 196616 | tf_op jit(solution)/shard_map/ppermute | solution.py:334
  10.2 2.7 %collective-permute-start.5 = (bf16[256,128]{1,0:T(8,128)(2,1)S(1)}, bf16[256,128]{1,0:T(8,128)(2,1)S(1)}, u32[]{:S(2)}, u32[]{:S(2)}) collective-permute-start(bf16[256,128]{1,0:T(8,128)(2,1)S(1)} %get-tuple-element.30.rest_0_), channel_id=1, source_target_pairs={{24,0},{16,8},{8,16},{0,24},{25,1},{17,9},{9,17},{1,25},{26,2},{18... | collective-permute-start | bytes 196616 | tf_op jit(solution)/shard_map/ppermute | solution.py:315
  12.9 0.4 collective-permute-start.4
  13.3 1.2 %collective-permute-start.3 = (bf16[256,128]{1,0:T(8,128)(2,1)S(1)}, bf16[256,128]{1,0:T(8,128)(2,1)S(1)}, u32[]{:S(2)}, u32[]{:S(2)}) collective-permute-start(bf16[256,128]{1,0:T(8,128)(2,1)S(1)} %get-tuple-element.30.rest_0_), channel_id=1, source_target_pairs={{8,0},{0,8},{24,16},{16,24},{9,1},{1,9},{25,17},{17,25},{10,2},{2,... | collective-permute-start | bytes 196616 | tf_op jit(solution)/shard_map/ppermute | solution.py:315
  14.6 0.0 copy-done.2
  14.6 0.0 copy-done.3
  14.6 0.0 copy-done.4
  14.6 0.7 %shard_map.84 = (bf16[2,128,2048]{2,1,0:T(8,128)(2,1)S(1)}, bf16[2,128,2048]{2,1,0:T(8,128)(2,1)S(1)}) custom-call(s32[1,8]{1,0:T(1,128)S(1)} %bitcast.4, bf16[256,2048]{1,0:T(8,128)(2,1)S(1)} %copy-done.2, bf16[256,2048]{1,0:T(8,128)(2,1)S(1)} %copy-done.3), custom_call_target="tpu_custom_call" | custom-call | flops 67108864 | bytes 131072 | tf_op jit(solution)/shard_map/pallas_call | solution.py:286
  15.3 0.0 collective-permute-done.rest_1_
  15.3 0.0 collective-permute-done.2.rest_3_
  15.3 5.6 %shard_map.85 = (f32[5,256,2048]{2,1,0:T(8,128)S(1)}, f32[2,2048]{1,0:T(2,128)S(1)}, bf16[2,128,2048]{2,1,0:T(8,128)(2,1)S(1)}, bf16[1024,128]{1,0:T(8,128)(2,1)...) custom-call(s32[1,8]{1,0:T(1,128)S(1)} %bitcast.5, ...), custom_call_target="tpu_custom_call" | custom-call | flops 1342177280 | bytes 2621440 | tf_op jit(solution)/shard_map/pallas_call | solution.py:286
  21.0 0.9 %collective-permute-start.6 = (bf16[512,128]{1,0:T(8,128)(2,1)S(1)}, bf16[512,128]{1,0:T(8,128)(2,1)S(1)}, u32[]{:S(2)}, u32[]{:S(2)}) collective-permute-start(bf16[512,128]{1,0:T(8,128)(2,1)S(1)} %pad_maximum_fusion.1), channel_id=1, source_target_pairs={{8,0},{0,8},{24,16},{16,24},{9,1},{1,9},{25,17},{17,25},{10,2},{2,... | collective-permute-start | bytes 393224 | tf_op jit(solution)/shard_map/ppermute | solution.py:315
  21.9 0.0 collective-permute-done.5.rest_3_
  21.9 0.0 collective-permute-done.4.rest_2_
  21.9 0.0 collective-permute-done.3.rest_1_
  21.9 5.3 %shard_map.86 = (bf16[256,2048]{1,0:T(8,128)(2,1)}, bf16[5,256,2048]{2,1,0:T(8,128)(2,1)S(1)}, bf16[256,128]{1,0:T(8,128)(2,1)S(1)}, bf16[256,128]{1,0:T(8,128)(...) custom-call(s32[1,8]{1,0:T(1,128)S(1)} %bitcast.6, f32[5,256,2048]{2,1,0:T(8,128)S(1)} %get-tuple-element.27.p_ref, ...), custom_call_target="tpu_custom_call" | custom-call | flops 2013265920 | bytes 3932160 | tf_op jit(solution)/shard_map/pallas_call | solution.py:286
  27.2 0.0 copy-start
  27.2 2.3 %copy-done = bf16[5,256,2048]{2,1,0:T(8,128)(2,1)} copy-done((bf16[5,256,2048]{2,1,0:T(8,128)(2,1)}, bf16[5,256,2048]{2,1,0:T(8,128)(2,1)S(1)}, u32[]{:S(2)}) %copy-start) | copy-done | bytes 5242904
  29.5 0.0 collective-permute-done.6
  29.5 2.6 %collective-permute-start.7 = (bf16[512,128]{1,0:T(8,128)(2,1)S(1)}, bf16[512,128]{1,0:T(8,128)(2,1)S(1)}, u32[]{:S(2)}, u32[]{:S(2)}) collective-permute-start(bf16[512,128]{1,0:T(8,128)(2,1)S(1)} %pad_maximum_fusion.2), channel_id=1, source_target_pairs={{16,0},{24,8},{0,16},{8,24},{17,1},{25,9},{1,17},{9,25},{18,2},{26... | collective-permute-start | bytes 393224 | tf_op jit(solution)/shard_map/ppermute | solution.py:315
  32.1 1.0 %collective-permute-start.8 = (bf16[256,128]{1,0:T(8,128)(2,1)S(1)}, bf16[256,128]{1,0:T(8,128)(2,1)S(1)}, u32[]{:S(2)}, u32[]{:S(2)}) collective-permute-start(bf16[256,128]{1,0:T(8,128)(2,1)S(1)} %get-tuple-element.39), channel_id=1, source_target_pairs={{8,0},{0,8},{24,16},{16,24},{9,1},{1,9},{25,17},{17,25},{10,2},{2,... | collective-permute-start | bytes 196616 | tf_op jit(solution)/shard_map/ppermute | solution.py:315
  33.1 0.9 %collective-permute-start.9 = (bf16[256,128]{1,0:T(8,128)(2,1)S(1)}, bf16[256,128]{1,0:T(8,128)(2,1)S(1)}, u32[]{:S(2)}, u32[]{:S(2)}) collective-permute-start(bf16[256,128]{1,0:T(8,128)(2,1)S(1)} %get-tuple-element.40), channel_id=1, source_target_pairs={{24,0},{16,8},{8,16},{0,24},{25,1},{17,9},{9,17},{1,25},{26,2},{18... | collective-permute-start | bytes 196616 | tf_op jit(solution)/shard_map/ppermute | solution.py:315
  34.0 2.9 %collective-permute-done.8 = bf16[256,128]{1,0:T(8,128)(2,1)S(1)} collective-permute-done((bf16[256,128]{1,0:T(8,128)(2,1)S(1)}, bf16[256,128]{1,0:T(8,128)(2,1)S(1)}, u32[]{:S(2)}, u32[]{:S(2)}) %collective-permute-start.8) | collective-permute-done | bytes 65568 | tf_op jit(solution)/shard_map/ppermute | solution.py:315
  36.9 2.4 %collective-permute-done.9 = bf16[256,128]{1,0:T(8,128)(2,1)S(1)} collective-permute-done((bf16[256,128]{1,0:T(8,128)(2,1)S(1)}, bf16[256,128]{1,0:T(8,128)(2,1)S(1)}, u32[]{:S(2)}, u32[]{:S(2)}) %collective-permute-start.9) | collective-permute-done | bytes 65568 | tf_op jit(solution)/shard_map/ppermute | solution.py:315
  39.2 0.2 collective-permute-done.7
  39.4 0.1 add_convert_fusion.1
  39.5 0.7 %pad_maximum_fusion.3 = bf16[256,256]{1,0:T(8,128)(2,1)} fusion(bf16[256,128]{1,0:T(8,128)(2,1)S(1)} %get-tuple-element.45, bf16[256,128]{1,0:T(8,128)(2,1)S(1)} %get-tuple-element.44), kind=kLoop, calls=%fused_computation.3 | loop fusion | flops 262144 | bytes 262144 | tf_op jit(solution)/shard_map/concatenate | solution.py:378
  40.2 3.7 %all-to-all-start = ((bf16[8,32,256]{2,1,0:T(8,128)(2,1)}), bf16[8,32,256]{2,1,0:T(8,128)(2,1)S(1)}, u32[]{:S(2)}, u32[]{:S(2)}) async-start(bf16[8,32,256]{2,1,0:T(8,128)(2,1)} %bitcast.1), calls=%async_computation | async-start | bytes 262144 | tf_op jit(solution)/shard_map/all_to_all | solution.py:379
  43.9 0.0 copy-start.1
  43.9 2.5 %copy-done.1 = bf16[5,256,2048]{2,1,0:T(8,128)(2,1)S(1)} copy-done((bf16[5,256,2048]{2,1,0:T(8,128)(2,1)S(1)}, bf16[5,256,2048]{2,1,0:T(8,128)(2,1)}, u32[]{:S(2)}) %copy-start.1) | copy-done | bytes 5242904
  46.4 2.2 %shard_map.87 = bf16[256,2048]{1,0:T(8,128)(2,1)} custom-call(s32[1,8]{1,0:T(1,128)S(1)} %bitcast.7, bf16[5,256,2048]{2,1,0:T(8,128)(2,1)S(1)} %copy-done.1, bf16[1024,128]{1,0:T(8,128)(2,1)S(1)} %get-tuple-element.33.k_ref), custom_call_target="tpu_custom_call" | custom-call | flops 671088640 | bytes 1310720 | tf_op jit(solution)/shard_map/pallas_call | solution.py:286
  48.5 0.8 %all-to-all-done = bf16[8,32,256]{2,1,0:T(8,128)(2,1)S(1)} async-done(((bf16[8,32,256]{2,1,0:T(8,128)(2,1)}), bf16[8,32,256]{2,1,0:T(8,128)(2,1)S(1)}, u32[]{:S(2)}, u32[]{:S(2)}) %all-to-all-start) | async-done | bytes 131104 | tf_op jit(solution)/shard_map/all_to_all | solution.py:379
  49.4 0.7 %total.1 = (bf16[32,1024]{1,0:T(8,128)(2,1)}, bf16[32,1024]{1,0:T(8,128)(2,1)}) custom-call(bf16[8,1,32,256]{3,2,1,0:T(8,128)(2,1)S(1)} %bitcast.3), custom_call_target="tpu_custom_call" | custom-call | tf_op jit(solution)/shard_map/total/pallas_call | solution.py:398
  (5 shorter events, 0.1 us)
Async XLA Ops:
  1.6 13.0 %copy-start.2 = (bf16[256,2048]{1,0:T(8,128)(2,1)S(1)}, bf16[256,2048]{1,0:T(8,128)(2,1)}, u32[]{:S(2)}) copy-start(bf16[256,2048]{1,0:T(8,128)(2,1)} %q_ref.1) | copy-start | bytes 3145732
  1.6 13.0 %copy-start.3 = (bf16[256,2048]{1,0:T(8,128)(2,1)S(1)}, bf16[256,2048]{1,0:T(8,128)(2,1)}, u32[]{:S(2)}) copy-start(bf16[256,2048]{1,0:T(8,128)(2,1)} %g_ref.1) | copy-start | bytes 3145732
  1.6 13.0 %copy-start.4 = (s32[8]{0:T(128)S(1)}, s32[8]{0:T(128)}, u32[]{:S(2)}) copy-start(s32[8]{0:T(128)} %param.9) | copy-start | bytes 100
  1.6 7.2 %collective-permute-start.1 = (bf16[256,128]{1,0:T(8,128)(2,1)S(1)}, bf16[256,128]{1,0:T(8,128)(2,1)S(1)}, u32[]{:S(2)}, u32[]{:S(2)}) collective-permute-start(bf16[256,128]{1,0:T(8,128)(2,1)S(1)} %get-tuple-element.26.rest_0_), channel_id=1, source_target_pairs={{16,0},{24,8},{0,16},{8,24},{17,1},{25,9},{1,17},{9,25},{18,2},{26... | collective-permute-start | bytes 196616 | tf_op jit(solution)/shard_map/ppermute | solution.py:315
  5.7 9.6 %collective-permute-start = (bf16[256,128]{1,0:T(8,128)(2,1)S(1)}, bf16[256,128]{1,0:T(8,128)(2,1)S(1)}, u32[]{:S(2)}, u32[]{:S(2)}) collective-permute-start(bf16[256,128]{1,0:T(8,128)(2,1)S(1)} %get-tuple-element.26.rest_0_), channel_id=1, source_target_pairs={{8,0},{0,8},{24,16},{16,24},{9,1},{1,9},{25,17},{17,25},{10,2},{2,... | collective-permute-start | bytes 196616 | tf_op jit(solution)/shard_map/ppermute | solution.py:315
  8.8 6.5 %collective-permute-start.2 = (bf16[256,128]{1,0:T(8,128)(2,1)S(1)}, bf16[256,128]{1,0:T(8,128)(2,1)S(1)}, u32[]{:S(2)}, u32[]{:S(2)}) collective-permute-start(bf16[256,128]{1,0:T(8,128)(2,1)S(1)} %collective-permute-done.1.rest_2_), channel_id=1, source_target_pairs={{8,0},{0,8},{24,16},{16,24},{9,1},{1,9},{25,17},{17,25},{10,2},{2,... | collective-permute-start | bytes 196616 | tf_op jit(solution)/shard_map/ppermute | solution.py:334
  10.2 11.7 %collective-permute-start.5 = (bf16[256,128]{1,0:T(8,128)(2,1)S(1)}, bf16[256,128]{1,0:T(8,128)(2,1)S(1)}, u32[]{:S(2)}, u32[]{:S(2)}) collective-permute-start(bf16[256,128]{1,0:T(8,128)(2,1)S(1)} %get-tuple-element.30.rest_0_), channel_id=1, source_target_pairs={{24,0},{16,8},{8,16},{0,24},{25,1},{17,9},{9,17},{1,25},{26,2},{18... | collective-permute-start | bytes 196616 | tf_op jit(solution)/shard_map/ppermute | solution.py:315
  12.9 9.0 %collective-permute-start.4 = (bf16[256,128]{1,0:T(8,128)(2,1)S(1)}, bf16[256,128]{1,0:T(8,128)(2,1)S(1)}, u32[]{:S(2)}, u32[]{:S(2)}) collective-permute-start(bf16[256,128]{1,0:T(8,128)(2,1)S(1)} %get-tuple-element.30.rest_0_), channel_id=1, source_target_pairs={{16,0},{24,8},{0,16},{8,24},{17,1},{25,9},{1,17},{9,25},{18,2},{26... | collective-permute-start | bytes 196616 | tf_op jit(solution)/shard_map/ppermute | solution.py:315
  13.3 8.5 %collective-permute-start.3 = (bf16[256,128]{1,0:T(8,128)(2,1)S(1)}, bf16[256,128]{1,0:T(8,128)(2,1)S(1)}, u32[]{:S(2)}, u32[]{:S(2)}) collective-permute-start(bf16[256,128]{1,0:T(8,128)(2,1)S(1)} %get-tuple-element.30.rest_0_), channel_id=1, source_target_pairs={{8,0},{0,8},{24,16},{16,24},{9,1},{1,9},{25,17},{17,25},{10,2},{2,... | collective-permute-start | bytes 196616 | tf_op jit(solution)/shard_map/ppermute | solution.py:315
  21.0 8.5 %collective-permute-start.6 = (bf16[512,128]{1,0:T(8,128)(2,1)S(1)}, bf16[512,128]{1,0:T(8,128)(2,1)S(1)}, u32[]{:S(2)}, u32[]{:S(2)}) collective-permute-start(bf16[512,128]{1,0:T(8,128)(2,1)S(1)} %pad_maximum_fusion.1), channel_id=1, source_target_pairs={{8,0},{0,8},{24,16},{16,24},{9,1},{1,9},{25,17},{17,25},{10,2},{2,... | collective-permute-start | bytes 393224 | tf_op jit(solution)/shard_map/ppermute | solution.py:315
  27.2 2.3 %copy-start = (bf16[5,256,2048]{2,1,0:T(8,128)(2,1)}, bf16[5,256,2048]{2,1,0:T(8,128)(2,1)S(1)}, u32[]{:S(2)}) copy-start(bf16[5,256,2048]{2,1,0:T(8,128)(2,1)S(1)} %get-tuple-element.32.ds_ref) | copy-start | bytes 15728644
  29.5 9.9 %collective-permute-start.7 = (bf16[512,128]{1,0:T(8,128)(2,1)S(1)}, bf16[512,128]{1,0:T(8,128)(2,1)S(1)}, u32[]{:S(2)}, u32[]{:S(2)}) collective-permute-start(bf16[512,128]{1,0:T(8,128)(2,1)S(1)} %pad_maximum_fusion.2), channel_id=1, source_target_pairs={{16,0},{24,8},{0,16},{8,24},{17,1},{25,9},{1,17},{9,25},{18,2},{26... | collective-permute-start | bytes 393224 | tf_op jit(solution)/shard_map/ppermute | solution.py:315
  32.1 4.8 %collective-permute-start.8 = (bf16[256,128]{1,0:T(8,128)(2,1)S(1)}, bf16[256,128]{1,0:T(8,128)(2,1)S(1)}, u32[]{:S(2)}, u32[]{:S(2)}) collective-permute-start(bf16[256,128]{1,0:T(8,128)(2,1)S(1)} %get-tuple-element.39), channel_id=1, source_target_pairs={{8,0},{0,8},{24,16},{16,24},{9,1},{1,9},{25,17},{17,25},{10,2},{2,... | collective-permute-start | bytes 196616 | tf_op jit(solution)/shard_map/ppermute | solution.py:315
  33.1 6.2 %collective-permute-start.9 = (bf16[256,128]{1,0:T(8,128)(2,1)S(1)}, bf16[256,128]{1,0:T(8,128)(2,1)S(1)}, u32[]{:S(2)}, u32[]{:S(2)}) collective-permute-start(bf16[256,128]{1,0:T(8,128)(2,1)S(1)} %get-tuple-element.40), channel_id=1, source_target_pairs={{24,0},{16,8},{8,16},{0,24},{25,1},{17,9},{9,17},{1,25},{26,2},{18... | collective-permute-start | bytes 196616 | tf_op jit(solution)/shard_map/ppermute | solution.py:315
  40.2 9.2 %all-to-all-start = ((bf16[8,32,256]{2,1,0:T(8,128)(2,1)}), bf16[8,32,256]{2,1,0:T(8,128)(2,1)S(1)}, u32[]{:S(2)}, u32[]{:S(2)}) async-start(bf16[8,32,256]{2,1,0:T(8,128)(2,1)} %bitcast.1), calls=%async_computation | async-start | bytes 262144 | tf_op jit(solution)/shard_map/all_to_all | solution.py:379
  43.9 2.5 %copy-start.1 = (bf16[5,256,2048]{2,1,0:T(8,128)(2,1)S(1)}, bf16[5,256,2048]{2,1,0:T(8,128)(2,1)}, u32[]{:S(2)}) copy-start(bf16[5,256,2048]{2,1,0:T(8,128)(2,1)} %copy-done) | copy-start | bytes 15728644
